TPU v7x, 32 devices: a whole 2x2x4 slice. The times are simulated.
32 devices in a mesh: dp: 2 (over y), row: 4 (over x, core), col: 4 (over z).
Axes of the slice: x: 2, y: 2, z: 4, core: 2. Of those that a mesh axis runs over, the one named last changes fastest.
Arguments:
- tokens: bfloat16 [2048, 4096], P(('col', 'row'), 'dp'), may hold values from -6 to 6
- segments: int32 [4096], P('dp'), may hold values from 0 to 12, never falling along the last dimension, each value on 1 to 800 neighbouring positions
- channel_table: bfloat16 [14, 2048], P(None, ('col', 'row')), may hold values from -7.6 to 2
- w_recept: bfloat16 [4, 512, 2048], P(None, 'row', 'col'), may hold values from -0.125 to 0.125
- w_key: bfloat16 [4, 512, 2048], P(None, 'row', 'col'), may hold values from -0.125 to 0.125
- w_value: bfloat16 [4, 512, 2048], P(None, 'row', 'col'), may hold values from -0.125 to 0.125
- w_gate: bfloat16 [4, 512, 2048], P(None, 'row', 'col'), may hold values from -0.125 to 0.125
- w_output: bfloat16 [4, 512, 2048], P(None, 'row', 'col'), may hold values from -0.125 to 0.125
- ffn_key: bfloat16 [4, 1792, 2048], P(None, 'row', 'col'), may hold values from -0.125 to 0.125
- ffn_value: bfloat16 [4, 512, 7168], P(None, 'row', 'col'), may hold values from -0.0625 to 0.0625
- ffn_recept: bfloat16 [4, 512, 2048], P(None, 'row', 'col'), may hold values from -0.125 to 0.125
- cotangent: bfloat16 [2048, 4096], P(('col', 'row'), 'dp'), may hold values from -6 to 6
Outputs:
- mixed: bfloat16 [2048, 4096], P(('col', 'row'), 'dp')
- grad_tokens: float32 [2048, 4096], P(('col', 'row'), 'dp')
- grad_table: float32 [14, 2048], P(None, ('col', 'row'))
- grad_recept: float32 [4, 512, 2048], P(None, 'row', 'col')
- grad_key: float32 [4, 512, 2048], P(None, 'row', 'col')
- grad_value: float32 [4, 512, 2048], P(None, 'row', 'col')
- grad_gate: float32 [4, 512, 2048], P(None, 'row', 'col')
- grad_output: float32 [4, 512, 2048], P(None, 'row', 'col')
- grad_ffn_key: float32 [4, 1792, 2048], P(None, 'row', 'col')
- grad_ffn_value: float32 [4, 512, 7168], P(None, 'row', 'col')
- grad_ffn_recept: float32 [4, 512, 2048], P(None, 'row', 'col')
Inputs may be any that keep to these rules, and one draw needn't show every extreme that they name: `segments`: numbers never fall along the tokens; each document holds 1 to 800 tokens and one holds exactly 800; a document may run past a sequence's end.
All inputs are finite; a program needn't handle non-finite values.
Results may differ from a plain program's by a relative error of at most 0.019.
Values may be sent and summed in bfloat16 or wider, within the bound.
No kernel may reach another device: no remote copies, remote signals or barrier semaphores. Data moves between devices by JAX's collectives and lax.ppermute only.
A program may use at most 192 MiB of HBM per device.

v0:
```python
import jax
import jax.numpy as jnp
from jax import lax
from jax.sharding import PartitionSpec as P

D = 2048
CHANNELS_PER_ATTN = 64
SEQ = 1024


exact_mode = lax.Precision.HIGHEST
norm_eps = 1e-05
group_eps = 0.00064
head_divisor = 8.0
block_len = 64


def feature_sums(stacked):
    return lax.psum(stacked, ("row", "col"))


def norm_forward(payload_entries, gain, bias):
    center = feature_sums(jnp.sum(payload_entries, axis=1)[None])[0] / D
    spread = (
        feature_sums(jnp.sum(jnp.square(payload_entries - center[:, None]), axis=1)[None])[0] / D
    )
    inverse = lax.rsqrt(spread + norm_eps)
    unit_normal = (payload_entries - center[:, None]) * inverse[:, None]
    return (unit_normal * gain + bias, unit_normal, inverse)


def norm_backward(grad_out, unit_normal, inverse, gain):
    grad_unit = grad_out * gain
    totals = feature_sums(
        jnp.stack([jnp.sum(grad_unit, axis=1), jnp.sum(grad_unit * unit_normal, axis=1)])
    )
    grad_in = inverse[:, None] * (
        grad_unit - totals[0][:, None] / D - unit_normal * totals[1][:, None] / D
    )
    return (grad_in, jnp.sum(grad_out * unit_normal, axis=0), jnp.sum(grad_out, axis=0))


def shift_down(payload_entries, handed_onward):
    earlier = jnp.concatenate([jnp.zeros_like(payload_entries[:1]), payload_entries[:-1]], axis=0)
    return earlier * handed_onward[:, None]


def mix_inputs(normed, coeffs, handed_onward):
    shifted = shift_down(normed, handed_onward)
    return normed[None] * coeffs[:, None, :] + shifted[None] * (1.0 - coeffs[:, None, :])


def attention_mixing_segmented(
    ongoing_memory_matrix, segment_portions, logarithmic_fading_speed, extra_current_coeffs
):
    acceptance_entries, lookup_sources, payload_entries, beginning_markers = segment_portions
    positions = jnp.arange(block_len, dtype=jnp.int32)
    start_marks = jnp.where(beginning_markers > 0.5, positions, -1)
    last_start = lax.cummax(start_marks, axis=0)
    steps_in = positions.astype(jnp.float32)[:, None, None]
    scaled_r = acceptance_entries * jnp.exp(logarithmic_fading_speed[None] * steps_in)
    scaled_k = lookup_sources * jnp.exp(-logarithmic_fading_speed[None] * (steps_in + 1.0))
    end_k = lookup_sources * jnp.exp(logarithmic_fading_speed[None] * (block_len - 1.0 - steps_in))
    allowed = (positions[:, None] > positions[None, :]) & (
        last_start[:, None] <= positions[None, :]
    )
    scores = jnp.einsum("thi,shi->hts", scaled_r, scaled_k, precision=exact_mode)
    scores = jnp.where(allowed[None], scores, 0.0)
    intra_term = jnp.einsum("hts,shj->thj", scores, payload_entries, precision=exact_mode)
    diagonal_contribution = (
        jnp.sum(
            acceptance_entries * extra_current_coeffs[None] * lookup_sources, axis=2, keepdims=True
        )
        * payload_entries
    )
    open_start = (last_start < 0).astype(jnp.float32)
    inter_term = (
        jnp.einsum("thi,hij->thj", scaled_r, ongoing_memory_matrix, precision=exact_mode)
        * open_start[:, None, None]
    )
    tail_mask = (positions >= last_start[block_len - 1]).astype(jnp.float32)
    fresh_sum = jnp.einsum(
        "shi,shj->hij", end_k * tail_mask[:, None, None], payload_entries, precision=exact_mode
    )
    carried = (
        ongoing_memory_matrix
        * jnp.exp(logarithmic_fading_speed * block_len)[:, :, None]
        * open_start[block_len - 1]
        + fresh_sum
    )
    return (carried, intra_term + diagonal_contribution + inter_term)


def attention_mixing_complete(
    acceptance_entries,
    lookup_sources,
    payload_entries,
    beginning_markers,
    logarithmic_fading_speed,
    extra_current_coeffs,
):
    block_count = acceptance_entries.shape[0] // block_len

    def reshaped(array_in):
        return array_in.reshape((block_count, block_len) + array_in.shape[1:])

    checked_outcome = jax.checkpoint(attention_mixing_segmented)

    def step_fn(ongoing_memory_matrix, segment_portions):
        return checked_outcome(
            ongoing_memory_matrix, segment_portions, logarithmic_fading_speed, extra_current_coeffs
        )

    initial = jnp.zeros(
        (
            logarithmic_fading_speed.shape[0],
            logarithmic_fading_speed.shape[1],
            logarithmic_fading_speed.shape[1],
        ),
        jnp.float32,
    )
    unused, outputs = lax.scan(
        step_fn,
        initial,
        (
            reshaped(acceptance_entries),
            reshaped(lookup_sources),
            reshaped(payload_entries),
            reshaped(beginning_markers),
        ),
    )
    return outputs.reshape(acceptance_entries.shape)


def time_block(projected, incoming_entries, handed_onward):
    unit_width = projected.shape[1] // 4
    attention_group_total = unit_width // CHANNELS_PER_ATTN
    token_count = projected.shape[0]

    def divide_attention_groups(array_in):
        return array_in.reshape(token_count, attention_group_total, CHANNELS_PER_ATTN)

    acceptance_entries = divide_attention_groups(projected[:, :unit_width])
    lookup_sources = divide_attention_groups(projected[:, unit_width : 2 * unit_width])
    payload_entries = divide_attention_groups(projected[:, 2 * unit_width : 3 * unit_width])
    gate_pre = projected[:, 3 * unit_width :]
    logarithmic_fading_speed = (-jnp.exp(incoming_entries[0])).reshape(
        attention_group_total, CHANNELS_PER_ATTN
    )
    extra_current_coeffs = incoming_entries[1].reshape(attention_group_total, CHANNELS_PER_ATTN)
    combined_attention_groups = (
        attention_mixing_complete(
            acceptance_entries,
            lookup_sources,
            payload_entries,
            1.0 - handed_onward,
            logarithmic_fading_speed,
            extra_current_coeffs,
        )
        / head_divisor
    )
    center = jnp.mean(combined_attention_groups, axis=2, keepdims=True)
    spread = jnp.mean(jnp.square(combined_attention_groups - center), axis=2, keepdims=True)
    grouped = ((combined_attention_groups - center) * lax.rsqrt(spread + group_eps)).reshape(
        token_count, unit_width
    )
    return (grouped * incoming_entries[2] + incoming_entries[3]) * jax.nn.silu(gate_pre)


def project_forward(stack_in, weights):
    gathered = lax.all_gather(stack_in, "row", axis=2, tiled=True)
    partials = [
        jnp.einsum(
            "tk,cwk->tcw", gathered[number], weights[number], preferred_element_type=jnp.float32
        )
        for number in range(len(weights))
    ]
    joined = jnp.concatenate(partials, axis=2)
    summed = lax.psum_scatter(joined, "col", scatter_dimension=1, tiled=True)
    return (gathered, summed[:, 0, :])


def project_backward(grad_out, gathered, weights):
    spread_out = lax.all_gather(grad_out[:, None, :], "col", axis=1, tiled=True)
    offset = 0
    grads_w = []
    grads_in = []
    for number in range(len(weights)):
        columns = weights[number].shape[1]
        block_grad = spread_out[:, :, offset : offset + columns]
        grads_w.append(
            jnp.einsum(
                "tk,tcw->cwk", gathered[number], block_grad, preferred_element_type=jnp.float32
            )
        )
        grads_in.append(
            jnp.einsum(
                "tcw,cwk->tk", block_grad, weights[number], preferred_element_type=jnp.float32
            )
        )
        offset = offset + columns
    summed = lax.psum_scatter(
        jnp.stack(grads_in).astype(jnp.bfloat16), "row", scatter_dimension=2, tiled=True
    ).astype(jnp.float32)
    return (summed, grads_w)


def run_forward(tokens_f, parameter_catalog, weights, handed_onward):
    w_recept, w_key, w_value, w_gate, w_output, ffn_key, ffn_value, ffn_recept = weights
    normed_one, unit_one, inverse_one = norm_forward(
        tokens_f, parameter_catalog[0], parameter_catalog[1]
    )
    mixes_one = mix_inputs(normed_one, parameter_catalog[2:6], handed_onward).astype(jnp.bfloat16)
    gathered_one, projected = project_forward(mixes_one, (w_recept, w_key, w_value, w_gate))
    gated_out = time_block(projected, parameter_catalog[6:10], handed_onward).astype(jnp.bfloat16)
    gathered_gated, branch = project_forward(gated_out[None], (w_output,))
    residual = tokens_f + branch
    normed_two, unit_two, inverse_two = norm_forward(
        residual, parameter_catalog[10], parameter_catalog[11]
    )
    mixes_two = mix_inputs(normed_two, parameter_catalog[12:14], handed_onward).astype(jnp.bfloat16)
    gathered_two, key_recept = project_forward(mixes_two, (ffn_key, ffn_recept))
    hidden_width = ffn_key.shape[1]
    hidden_pre = key_recept[:, :hidden_width]
    recept_pre = key_recept[:, hidden_width:]
    activated = jnp.square(jax.nn.relu(hidden_pre)).astype(jnp.bfloat16)
    gathered_act, payload_mapped = project_forward(activated[None], (ffn_value,))
    output = residual + jax.nn.sigmoid(recept_pre) * payload_mapped
    kept_state = (
        normed_one,
        unit_one,
        inverse_one,
        gathered_one,
        projected,
        gathered_gated,
        normed_two,
        unit_two,
        inverse_two,
        gathered_two,
        hidden_pre,
        recept_pre,
        gathered_act,
        payload_mapped,
    )
    return (output, kept_state)


def shards(
    tokens,
    segments,
    channel_table,
    w_recept,
    w_key,
    w_value,
    w_gate,
    w_output,
    ffn_key,
    ffn_value,
    ffn_recept,
    cotangent,
):
    tokens_f = tokens.astype(jnp.float32).T
    upstream = cotangent.astype(jnp.float32).T
    positions = jnp.arange(tokens_f.shape[0], dtype=jnp.int32)
    earlier = jnp.concatenate([segments[:1], segments[:-1]])
    handed_onward = 1.0 - ((positions % SEQ == 0) | (segments != earlier)).astype(jnp.float32)
    parameter_catalog = channel_table.astype(jnp.float32)
    weights = (w_recept, w_key, w_value, w_gate, w_output, ffn_key, ffn_value, ffn_recept)
    output, unused = run_forward(tokens_f, parameter_catalog, weights, handed_onward)
    tokens_again, upstream, output = lax.optimization_barrier((tokens_f, upstream, output))
    unused_out, kept_state = run_forward(tokens_again, parameter_catalog, weights, handed_onward)
    (
        normed_one,
        unit_one,
        inverse_one,
        gathered_one,
        projected,
        gathered_gated,
        normed_two,
        unit_two,
        inverse_two,
        gathered_two,
        hidden_pre,
        recept_pre,
        gathered_act,
        payload_mapped,
    ) = kept_state
    gate_value = jax.nn.sigmoid(recept_pre)
    grad_valued = (upstream * gate_value).astype(jnp.bfloat16)
    grad_recept = upstream * payload_mapped * gate_value * (1.0 - gate_value)
    grad_act, grads_value = project_backward(grad_valued, gathered_act, (ffn_value,))
    grad_hidden = grad_act[0] * 2.0 * jax.nn.relu(hidden_pre)
    grad_key_recept = jnp.concatenate([grad_hidden, grad_recept], axis=1).astype(jnp.bfloat16)
    grad_mixes_two, grads_ffn = project_backward(
        grad_key_recept, gathered_two, (ffn_key, ffn_recept)
    )
    unused_two, second_pull = jax.vjp(
        lambda normed, coeffs: mix_inputs(normed, coeffs, handed_onward),
        normed_two,
        parameter_catalog[12:14],
    )
    grad_normed_two, grad_coeff_two = second_pull(grad_mixes_two)
    grad_res_norm, gain_two, bias_two = norm_backward(
        grad_normed_two, unit_two, inverse_two, parameter_catalog[10]
    )
    grad_residual = upstream + grad_res_norm
    grad_gated, grads_output = project_backward(
        grad_residual.astype(jnp.bfloat16), gathered_gated, (w_output,)
    )
    unused_block, block_pull = jax.vjp(
        lambda projected_in, incoming_entries: time_block(
            projected_in, incoming_entries, handed_onward
        ),
        projected,
        parameter_catalog[6:10],
    )
    grad_projected, grad_rows = block_pull(grad_gated[0])
    grad_mixes_one, grads_time = project_backward(
        grad_projected.astype(jnp.bfloat16), gathered_one, (w_recept, w_key, w_value, w_gate)
    )
    unused_one, first_pull = jax.vjp(
        lambda normed, coeffs: mix_inputs(normed, coeffs, handed_onward),
        normed_one,
        parameter_catalog[2:6],
    )
    grad_normed_one, grad_coeff_one = first_pull(grad_mixes_one)
    grad_tok_norm, gain_one, bias_one = norm_backward(
        grad_normed_one, unit_one, inverse_one, parameter_catalog[0]
    )
    grad_tokens = grad_residual + grad_tok_norm
    table_grad = jnp.concatenate(
        [
            gain_one[None],
            bias_one[None],
            grad_coeff_one,
            grad_rows,
            gain_two[None],
            bias_two[None],
            grad_coeff_two,
        ],
        axis=0,
    )
    summed = (
        lax.psum(grads_time[0].astype(jnp.bfloat16), "dp").astype(jnp.float32),
        lax.psum(grads_time[1].astype(jnp.bfloat16), "dp").astype(jnp.float32),
        lax.psum(grads_time[2].astype(jnp.bfloat16), "dp").astype(jnp.float32),
        lax.psum(grads_time[3].astype(jnp.bfloat16), "dp").astype(jnp.float32),
        lax.psum(grads_output[0].astype(jnp.bfloat16), "dp").astype(jnp.float32),
        lax.psum(grads_ffn[0].astype(jnp.bfloat16), "dp").astype(jnp.float32),
        lax.psum(grads_value[0].astype(jnp.bfloat16), "dp").astype(jnp.float32),
        lax.psum(grads_ffn[1].astype(jnp.bfloat16), "dp").astype(jnp.float32),
        lax.psum(table_grad.astype(jnp.bfloat16), "dp").astype(jnp.float32),
    )
    return (
        output.astype(jnp.bfloat16).T,
        grad_tokens.T,
        summed[8],
        summed[0],
        summed[1],
        summed[2],
        summed[3],
        summed[4],
        summed[5],
        summed[6],
        summed[7],
    )


def solution(mesh):
    in_specs = (
        P(("col", "row"), "dp"),
        P("dp"),
        P(None, ("col", "row")),
        P(None, "row", "col"),
        P(None, "row", "col"),
        P(None, "row", "col"),
        P(None, "row", "col"),
        P(None, "row", "col"),
        P(None, "row", "col"),
        P(None, "row", "col"),
        P(None, "row", "col"),
        P(("col", "row"), "dp"),
    )
    out_specs = (
        P(("col", "row"), "dp"),
        P(("col", "row"), "dp"),
        P(None, ("col", "row")),
        P(None, "row", "col"),
        P(None, "row", "col"),
        P(None, "row", "col"),
        P(None, "row", "col"),
        P(None, "row", "col"),
        P(None, "row", "col"),
        P(None, "row", "col"),
        P(None, "row", "col"),
    )
    return jax.shard_map(shards, mesh=mesh, in_specs=in_specs, out_specs=out_specs, check_vma=False)
```

profile of v0, /device:TPU:0, one launch (start us, length us, event | category | flops | bytes accessed | tf_op | source)
XLA Modules:
  0.0 4988.6 jit_solution(13791718364554033619)
XLA Ops:
  12.2 36.0 psum.133
  49.4 30.4 psum.134
  90.2 58.4 %all-gather.20.cloned.1.call-done = bf16[4,2048,512]{2,1,0:T(8,128)(2,1)} async-done(((bf16[4,2048,128]{2,1,0:T(8,128)(2,1)}), bf16[4,2048,512]{2,1,0:T(8,128)(2,1)}) %all-gather.20.cloned.1.call-update) | async-done | bytes 8388624 | tf_op jit(solution)/shard_map/all_gather | solution.py:171
  157.4 6.2 pad_maximum_fusion.2
  165.3 278.8 %reduce-scatter.17.cloned.1.call-done = f32[2048,1,512]{0,2,1:T(8,128)} async-done(((f32[2048,4,512]{0,2,1:T(8,128)}), f32[2048,1,512]{0,2,1:T(8,128)}) %reduce-scatter.17.cloned.1.call-update) | async-done | bytes 4194320 | tf_op jit(solution)/shard_map/reduce_scatter | solution.py:179
  457.3 281.5 %while.72 = (s32[]{:T(128)}, f32[2,64,64]{2,1,0:T(8,128)S(1)}, f32[32,64,2,64]{3,1,2,0:T(8,128)}, f32[2,64]{1,0:T(2,128)S(1)}, f32[32,64]{1,0:T(8,128)S(1)}, /*i...) while((s32[]{:T(128)}, f32[2,64,64]{2,1,0:T(8,128)S(1)}, ...), condition=%wide.region_8.9_spmd.clone, body=%wide.region_5.8_spmd.clone.sunk | while | flops 25355200 | bytes 1069532 | solution.py:122
  753.2 23.4 all-gather.30.cloned.1.call-done
  776.6 4.8 fusion.205
  782.2 76.1 %reduce-scatter.19.cloned.1.call-done = f32[2048,1,128]{0,2,1:T(8,128)} async-done(((f32[2048,4,128]{0,2,1:T(8,128)}), f32[2048,1,128]{0,2,1:T(8,128)}) %reduce-scatter.19.cloned.1.call-update) | async-done | bytes 1048592 | tf_op jit(solution)/shard_map/reduce_scatter | solution.py:179
  859.8 33.6 psum.135
  893.6 30.5 psum.136
  934.9 33.7 all-gather.22.cloned.1.call-done
  971.7 4.2 fusion.196
  975.9 7.0 pad_maximum_fusion
  983.0 313.9 %reduce-scatter.21.cloned.1.call-done = f32[2048,1,576]{0,2,1:T(8,128)} async-done(((f32[2048,4,576]{0,2,1:T(8,128)}), f32[2048,1,576]{0,2,1:T(8,128)}) %reduce-scatter.21.cloned.1.call-update) | async-done | bytes 4718608 | tf_op jit(solution)/shard_map/reduce_scatter | solution.py:179
  1300.7 53.5 %all-gather.32.cloned.1.call-done = bf16[2048,1792]{0,1:T(8,128)(2,1)} async-done(((bf16[2048,448]{0,1:T(8,128)(2,1)}), bf16[2048,1792]{0,1:T(8,128)(2,1)}) %all-gather.32.cloned.1.call-update) | async-done | bytes 7340048 | tf_op jit(solution)/shard_map/all_gather | solution.py:171
  1354.2 9.6 fusion.163
  1366.5 74.2 %reduce-scatter.23.cloned.1.call-done = f32[2048,1,128]{0,2,1:T(8,128)} async-done(((f32[2048,4,128]{0,2,1:T(8,128)}), f32[2048,1,128]{0,2,1:T(8,128)}) %reduce-scatter.23.cloned.1.call-update) | async-done | bytes 1048592 | tf_op jit(solution)/shard_map/reduce_scatter | solution.py:179
  1443.8 33.6 psum.137
  1477.5 30.5 psum.138
  1520.4 58.6 %all-gather.24.cloned.1.call-done = bf16[4,2048,512]{2,1,0:T(8,128)(2,1)} async-done(((bf16[4,2048,128]{2,1,0:T(8,128)(2,1)}), bf16[4,2048,512]{2,1,0:T(8,128)(2,1)}) %all-gather.24.cloned.1.call-update) | async-done | bytes 8388624 | tf_op jit(solution)/shard_map/all_gather | solution.py:171
  1587.7 6.2 pad_maximum_fusion.3
  1594.7 279.7 %reduce-scatter.25.cloned.1.call-done = f32[2048,1,512]{0,2,1:T(8,128)} async-done(((f32[2048,4,512]{0,2,1:T(8,128)}), f32[2048,1,512]{0,2,1:T(8,128)}) %reduce-scatter.25.cloned.1.call-update) | async-done | bytes 4194320 | tf_op jit(solution)/shard_map/reduce_scatter | solution.py:179
  1898.1 355.7 %while.73 = (s32[]{:T(128)}, f32[2,64,64]{2,1,0:T(8,128)S(1)}, f32[32,64,2,64]{3,1,2,0:T(8,128)}, f32[2,64]{1,0:T(2,128)S(1)}, f32[32,64]{1,0:T(8,128)}, /*index...) while((s32[]{:T(128)}, f32[2,64,64]{2,1,0:T(8,128)S(1)}, ...), condition=%wide.region_26.27_spmd.clone, body=%wide.region_23.26_spmd.clone.sunk | while | flops 25355200 | bytes 975315 | solution.py:122
  2255.4 331.4 %while.75 = (s32[]{:T(128)}, f32[2,64,64]{2,1,0:T(8,128)S(1)}, f32[32,64,2,64]{3,1,2,0:T(8,128)}, f32[32,2,64,64]{3,2,1,0:T(8,128)}, f32[2,64,1]{1,0,2:T(2,128)S...) while((s32[]{:T(128)}, f32[2,64,64]{2,1,0:T(8,128)S(1)}, ...), condition=%wide.region_46.47_spmd.clone.clone.clone.clone, body=%wide.region_43.46_spmd.clone.clone.clone.clone.sunk | while | flops 25362944 | bytes 1068772 | solution.py:122
  2603.3 23.4 all-gather.34.cloned.1.call-done
  2626.7 4.9 fusion.203
  2631.7 76.9 %reduce-scatter.27.cloned.1.call-done = f32[2048,1,128]{0,2,1:T(8,128)} async-done(((f32[2048,4,128]{0,2,1:T(8,128)}), f32[2048,1,128]{0,2,1:T(8,128)}) %reduce-scatter.27.cloned.1.call-update) | async-done | bytes 1048592 | tf_op jit(solution)/shard_map/reduce_scatter | solution.py:179
  2710.9 34.0 psum.139
  2746.2 30.5 psum.140
  2786.1 34.1 all-gather.26.cloned.1.call-done
  2827.5 7.0 pad_maximum_fusion.1
  2834.6 313.9 %reduce-scatter.29.cloned.1.call-done = f32[2048,1,576]{0,2,1:T(8,128)} async-done(((f32[2048,4,576]{0,2,1:T(8,128)}), f32[2048,1,576]{0,2,1:T(8,128)}) %reduce-scatter.29.cloned.1.call-update) | async-done | bytes 4718608 | tf_op jit(solution)/shard_map/reduce_scatter | solution.py:179
  3152.2 53.5 %all-gather.38.cloned.1.call-done = bf16[2048,1792]{0,1:T(8,128)(2,1)} async-done(((bf16[2048,448]{0,1:T(8,128)(2,1)}), bf16[2048,1792]{0,1:T(8,128)(2,1)}) %all-gather.38.cloned.1.call-update) | async-done | bytes 7340048 | tf_op jit(solution)/shard_map/all_gather | solution.py:171
  3205.7 9.5 fusion.161
  3215.3 76.9 %reduce-scatter.33.cloned.1.call-done = f32[2048,1,128]{0,2,1:T(8,128)} async-done(((f32[2048,4,128]{0,2,1:T(8,128)}), f32[2048,1,128]{0,2,1:T(8,128)}) %reduce-scatter.33.cloned.1.call-update) | async-done | bytes 1048592 | tf_op jit(solution)/shard_map/reduce_scatter | solution.py:179
  3295.2 46.4 all-gather.36.cloned.1.call-done
  3341.6 9.1 fusion.165
  3350.8 64.3 %reduce-scatter.31.cloned.1.call-done = bf16[1,2048,448]{1,2,0:T(8,128)(2,1)} async-done(((bf16[1,2048,1792]{1,2,0:T(8,128)(2,1)}), bf16[1,2048,448]{1,2,0:T(8,128)(2,1)}) %reduce-scatter.31.cloned.1.call-update) | async-done | bytes 1835024 | tf_op jit(solution)/shard_map/reduce_scatter | solution.py:202
  3420.1 166.9 %all-gather.28.cloned.1.call-done = bf16[2048,4,576]{0,2,1:T(8,128)(2,1)} async-done(((bf16[2048,1,576]{0,2,1:T(8,128)(2,1)}), bf16[2048,4,576]{0,2,1:T(8,128)(2,1)}) %all-gather.28.cloned.1.call-update) | async-done | bytes 9437200 | tf_op jit(solution)/shard_map/all_gather | solution.py:184
  3591.3 4.2 fusion.182
  3597.9 11.3 copy.376
  3609.3 6.7 copy.447
  3616.1 42.7 reduce-scatter.37.cloned.1.call-done
  3678.0 60.7 %psum.141 = f32[2,2048]{1,0:T(2,128)S(1)} all-reduce(f32[2,2048]{1,0:T(2,128)S(1)} %pad_maximum_fusion.7), channel_id=1, replica_groups=mesh['dp'=2,'row'=4,'col'=4] {'row','col'}, use_global_device_ids=true, to_apply=%region_42.43 | all-reduce | flops 4096 | bytes 32768 | tf_op jit(solution)/shard_map/psum | solution.py:19
  3741.5 44.3 all-gather.40.cloned.1.call-done
  3785.8 4.2 fusion.186
  3802.3 18.1 reduce-scatter.35.cloned.1.call-done
  3833.1 5.0 add_multiply_fusion
  3842.9 629.8 %while.74 = (s32[]{:T(128)}, f32[2,64]{1,0:T(2,128)S(1)}, f32[2,64]{1,0:T(2,128)S(1)}, f32[2,64,64]{2,1,0:T(8,128)S(1)}, f32[32,64,2,64]{1,0,3,2:T(8,128)}, /*in...) while((s32[]{:T(128)}, f32[2,64]{1,0:T(2,128)S(1)}, ...), condition=%wide.region_62.63_spmd.clone, body=%wide.region_53.62_spmd.clone.sunk | while | flops 57132356 | bytes 2100241 | solution.py:122
  4485.0 9.1 fusion.179
  4497.9 8.6 fusion.229
  4508.6 126.1 %all-gather.42.cloned.1.call-done = bf16[2048,2048]{0,1:T(8,128)(2,1)} async-done(((bf16[2048,512]{0,1:T(8,128)(2,1)}), bf16[2048,2048]{0,1:T(8,128)(2,1)}) %all-gather.42.cloned.1.call-update) | async-done | bytes 8388624 | tf_op jit(solution)/shard_map/all_gather | solution.py:184
  4634.7 4.4 fusion.244
  4639.1 4.4 fusion.241
  4664.8 15.2 copy.378
  4680.1 16.3 copy.448
  4697.2 119.0 %all-reduce.17.cloned.1.call-done = (bf16[4,128,512]{2,1,0:T(8,128)(2,1)}, bf16[4,128,512]{2,1,0:T(8,128)(2,1)}, bf16[4,128,512]{2,1,0:T(8,128)(2,1)}, bf16[4,12...) async-done(((bf16[4,128,512]{2,1,0:T(8,128)(2,1)}, ...) | async-done | bytes 6815760 | tf_op jit(solution)/shard_map/psum | solution.py:344
  4829.9 60.6 %reduce-scatter.39.cloned.1.call-done = bf16[128,8192]{1,0:T(8,128)(2,1)} async-done(((bf16[512,8192]{1,0:T(8,128)(2,1)}), bf16[128,8192]{1,0:T(8,128)(2,1)}) %reduce-scatter.39.cloned.1.call-update) | async-done | bytes 2097168
  4890.5 4.5 reshape.914
  4895.1 4.9 copy.379
  4900.0 4.4 fusion.172
  4912.4 60.7 %psum.142 = f32[2,2048]{1,0:T(2,128)S(1)} all-reduce(f32[2,2048]{1,0:T(2,128)S(1)} %pad_maximum_fusion.8), channel_id=1, replica_groups=mesh['dp'=2,'row'=4,'col'=4] {'row','col'}, use_global_device_ids=true, to_apply=%region_68.69 | all-reduce | flops 4096 | bytes 32768 | tf_op jit(solution)/shard_map/psum | solution.py:19
  4973.2 4.9 psum.143
  (3632 shorter events, 1886.0 us)
Async XLA Ops:
  7.2 964.5 %copy-start = (bf16[4,448,512]{2,1,0:T(8,128)(2,1)S(1)}, bf16[4,448,512]{2,1,0:T(8,128)(2,1)}, u32[]{:S(2)}) copy-start(bf16[4,448,512]{2,1,0:T(8,128)(2,1)} %param.28) | copy-start | bytes 5505028
  7.2 141.4 %all-gather.20.cloned.1.call-start = ((), (), s32[]{:S(2)}) async-start(), calls=%async_computation.12 | async-start | bytes 10485760 | tf_op jit(solution)/shard_map/all_gather | solution.py:171
  8.1 774.2 %copy-start.41 = (f32[14,128]{1,0:T(8,128)}, f32[14,128]{1,0:T(8,128)S(1)}, u32[]{:S(2)}) copy-start(f32[14,128]{1,0:T(8,128)S(1)} %convert_element_type.306) | copy-start | bytes 21508
  9.1 915.0 %copy-start.45 = (f32[128]{0:T(128)}, f32[128]{0:T(128)S(1)}, u32[]{:S(2)}) copy-start(f32[128]{0:T(128)S(1)} %get-tuple-element.1371) | copy-start | bytes 1540
  9.1 1499.0 %copy-start.43 = (f32[128]{0:T(128)}, f32[128]{0:T(128)S(1)}, u32[]{:S(2)}) copy-start(f32[128]{0:T(128)S(1)} %get-tuple-element.1369) | copy-start | bytes 1540
  9.1 1507.8 %copy-start.36 = (f32[4,128]{1,0:T(4,128)}, f32[4,128]{1,0:T(4,128)S(1)}, u32[]{:S(2)}) copy-start(f32[4,128]{1,0:T(4,128)S(1)} %broadcast_subtract_fusion.4) | copy-start | bytes 6148
  9.8 1507.1 %copy-start.38 = (f32[4,128]{1,0:T(4,128)}, f32[4,128]{1,0:T(4,128)S(1)}, u32[]{:S(2)}) copy-start(f32[4,128]{1,0:T(4,128)S(1)} %slice.306) | copy-start | bytes 6148
  48.1 34.3 copy-start.40
  90.2 353.9 %reduce-scatter.17.cloned.1.call-start = ((), (), s32[]{:S(2)}) async-start(), calls=%async_computation.13 | async-start | bytes 20971520 | tf_op jit(solution)/shard_map/reduce_scatter | solution.py:179
  148.6 6.2 copy-start.56
  163.7 613.0 %all-gather.30.cloned.1.call-start = ((), (), s32[]{:S(2)}) async-start(), calls=%async_computation.27 | async-start | bytes 2621440 | tf_op jit(solution)/shard_map/all_gather | solution.py:171
  738.9 5.6 copy-start.50
  750.4 26.3 copy-start.23
  753.2 105.2 %reduce-scatter.19.cloned.1.call-start = ((), (), s32[]{:S(2)}) async-start(), calls=%async_computation.14 | async-start | bytes 5242880 | tf_op jit(solution)/shard_map/reduce_scatter | solution.py:179
  781.4 76.9 %copy-start.4 = (bf16[128,2048]{1,0:T(8,128)(2,1)S(1)}, bf16[128,2048]{1,0:T(8,128)(2,1)}, u32[]{:S(2)}) copy-start(bf16[128,2048]{1,0:T(8,128)(2,1)} %param.20) | copy-start | bytes 1572868
  781.4 187.2 %all-gather.22.cloned.1.call-start = ((), (), s32[]{:S(2)}) async-start(), calls=%async_computation.15 | async-start | bytes 5242880 | tf_op jit(solution)/shard_map/all_gather | solution.py:171
  858.3 35.0 copy-start.6
  934.4 362.5 %reduce-scatter.21.cloned.1.call-start = ((), (), s32[]{:S(2)}) async-start(), calls=%async_computation.16 | async-start | bytes 23592960 | tf_op jit(solution)/shard_map/reduce_scatter | solution.py:179
  983.0 371.2 %all-gather.32.cloned.1.call-start = ((), (), s32[]{:S(2)}) async-start(), calls=%async_computation.28 | async-start | bytes 9175040 | tf_op jit(solution)/shard_map/all_gather | solution.py:171
  1300.6 140.1 %reduce-scatter.23.cloned.1.call-start = ((), (), s32[]{:S(2)}) async-start(), calls=%async_computation.17 | async-start | bytes 5242880 | tf_op jit(solution)/shard_map/reduce_scatter | solution.py:179
  1363.9 215.1 %all-gather.24.cloned.1.call-start = ((), (), s32[]{:S(2)}) async-start(), calls=%async_computation.18 | async-start | bytes 10485760 | tf_op jit(solution)/shard_map/all_gather | solution.py:171
  1364.0 1344.5 %copy-start.2 = (f32[2048,128]{0,1:T(8,128)}, f32[2048,128]{0,1:T(8,128)S(1)}, u32[]{:S(2)}) copy-start(f32[2048,128]{0,1:T(8,128)S(1)} %convert_bitcast_fusion) | copy-start | bytes 3145732
  1477.4 34.5 copy-start.32
  1520.3 58.6 %copy-start.63 = (bf16[4,128,512]{2,1,0:T(8,128)(2,1)S(1)}, bf16[4,128,512]{2,1,0:T(8,128)(2,1)}, u32[]{:S(2)}) copy-start(bf16[4,128,512]{2,1,0:T(8,128)(2,1)} %param.26) | copy-start | bytes 1572868
  1520.4 354.1 %reduce-scatter.25.cloned.1.call-start = ((), (), s32[]{:S(2)}) async-start(), calls=%async_computation.19 | async-start | bytes 20971520 | tf_op jit(solution)/shard_map/reduce_scatter | solution.py:179
  1579.0 6.1 copy-start.55
  1594.0 1032.7 %all-gather.34.cloned.1.call-start = ((), (), s32[]{:S(2)}) async-start(), calls=%async_computation.29 | async-start | bytes 2621440 | tf_op jit(solution)/shard_map/all_gather | solution.py:171
  2600.1 26.6 copy-start.24
  2603.2 105.3 %reduce-scatter.27.cloned.1.call-start = ((), (), s32[]{:S(2)}) async-start(), calls=%async_computation.20 | async-start | bytes 5242880 | tf_op jit(solution)/shard_map/reduce_scatter | solution.py:179
  2631.7 145.1 %copy-start.46 = (f32[128]{0:T(128)S(1)}, f32[128]{0:T(128)}, u32[]{:S(2)}) copy-start(f32[128]{0:T(128)} %copy-done.45) | copy-start | bytes 1540
  2631.7 188.6 %all-gather.26.cloned.1.call-start = ((), (), s32[]{:S(2)}) async-start(), calls=%async_computation.21 | async-start | bytes 5242880 | tf_op jit(solution)/shard_map/all_gather | solution.py:171
  2783.5 36.7 copy-start.61
  2786.1 362.4 %reduce-scatter.29.cloned.1.call-start = ((), (), s32[]{:S(2)}) async-start(), calls=%async_computation.22 | async-start | bytes 23592960 | tf_op jit(solution)/shard_map/reduce_scatter | solution.py:179
  2834.5 371.2 %all-gather.38.cloned.1.call-start = ((), (), s32[]{:S(2)}) async-start(), calls=%async_computation.31 | async-start | bytes 9175040 | tf_op jit(solution)/shard_map/all_gather | solution.py:171
  3152.2 140.0 %reduce-scatter.33.cloned.1.call-start = ((), (), s32[]{:S(2)}) async-start(), calls=%async_computation.24 | async-start | bytes 5242880 | tf_op jit(solution)/shard_map/reduce_scatter | solution.py:179
  3215.2 76.9 %copy-start.10 = (f32[2048,128]{0,1:T(8,128)S(1)}, f32[2048,128]{0,1:T(8,128)}, u32[]{:S(2)}) copy-start(f32[2048,128]{0,1:T(8,128)} %convert_bitcast_fusion.1) | copy-start | bytes 3145732
  3215.3 126.3 %all-gather.36.cloned.1.call-start = ((), (), s32[]{:S(2)}) async-start(), calls=%async_computation.30 | async-start | bytes 2621440 | tf_op jit(solution)/shard_map/all_gather | solution.py:184
  3295.0 120.1 %reduce-scatter.31.cloned.1.call-start = ((), (), s32[]{:S(2)}) async-start(), calls=%async_computation.23 | async-start | bytes 9175040 | tf_op jit(solution)/shard_map/reduce_scatter | solution.py:202
  3350.7 236.3 %all-gather.28.cloned.1.call-start = ((), (), s32[]{:S(2)}) async-start(), calls=%async_computation.25 | async-start | bytes 11796480 | tf_op jit(solution)/shard_map/all_gather | solution.py:184
  3420.0 167.0 %copy-start.62 = (bf16[4,128,512]{2,1,0:T(8,128)(2,1)S(1)}, bf16[4,128,512]{2,1,0:T(8,128)(2,1)}, u32[]{:S(2)}) copy-start(bf16[4,128,512]{2,1,0:T(8,128)(2,1)} %param.30) | copy-start | bytes 1572868
  3420.0 238.7 %reduce-scatter.37.cloned.1.call-start = ((), (), s32[]{:S(2)}) async-start(), calls=%async_computation.34 | async-start | bytes 5242880
  3587.0 4.3 copy-start.54
  3615.9 169.9 %all-gather.40.cloned.1.call-start = ((), (), s32[]{:S(2)}) async-start(), calls=%async_computation.32 | async-start | bytes 2621440 | tf_op jit(solution)/shard_map/all_gather | solution.py:184
  3616.1 49.0 copy-start.12
  3672.5 4.1 copy-start.5
  3738.6 47.2 copy-start.25
  3741.5 78.9 %reduce-scatter.35.cloned.1.call-start = ((), (), s32[]{:S(2)}) async-start(), calls=%async_computation.26 | async-start | bytes 2621440 | tf_op jit(solution)/shard_map/reduce_scatter | solution.py:202
  3790.1 844.6 %all-gather.42.cloned.1.call-start = ((), (), s32[]{:S(2)}) async-start(), calls=%async_computation.33 | async-start | bytes 10485760 | tf_op jit(solution)/shard_map/all_gather | solution.py:184
  4484.9 331.3 %all-reduce.17.cloned.1.call-start = ((), (), s32[]{:S(2)}) async-start(), calls=%async_computation.36 | async-start | bytes 13631488 | tf_op jit(solution)/shard_map/psum | solution.py:344
  4485.0 9.1 copy-start.58
  4497.9 8.6 copy-start.21
  4497.9 8.6 copy-start.60
  4634.7 8.8 slice-start
  4639.1 4.4 slice-start.1
  4650.8 4.1 copy-start.65
  4650.9 239.7 %reduce-scatter.39.cloned.1.call-start = ((), (), s32[]{:S(2)}) async-start(), calls=%async_computation.35 | async-start | bytes 10485760
  4651.9 6.4 slice-start.2
  4816.2 4.4 copy-start.31
  4816.2 5.5 copy-start.30
  4818.4 4.4 copy-start.29
  4895.0 4.9 copy-start.8
  4895.0 4.9 copy-start.9
  4895.0 4.9 copy-start.37
  4895.0 4.9 copy-start.39
  (39 other events, 93.9 us)
Sparse Core Ops, SparseCore 0:
  90.3 58.2 all-gather.19
  163.8 280.2 reduce-scatter.16
  753.3 23.2 all-gather.29
  781.6 76.7 reduce-scatter.18
  934.5 33.9 all-gather.21
  983.1 313.7 reduce-scatter.20
  1300.8 53.3 all-gather.31
  1364.0 76.7 reduce-scatter.22
  1520.5 58.4 all-gather.23
  1594.1 280.2 reduce-scatter.24
  2603.3 23.3 all-gather.33
  2631.8 76.7 reduce-scatter.26
  2786.2 33.9 all-gather.25
  2834.6 313.7 reduce-scatter.28
  3152.3 53.3 all-gather.37
  3215.4 76.7 reduce-scatter.32
  3295.1 46.4 all-gather.35
  3350.8 64.1 reduce-scatter.30
  3420.2 166.7 all-gather.27
  3616.1 42.6 reduce-scatter.36
  3741.6 44.1 all-gather.39
  3790.2 30.1 reduce-scatter.34
  4485.0 149.6 all-gather.41
  4651.0 165.1 all-reduce.16
  4818.8 71.7 reduce-scatter.38
where the time goes:
time: 5030 us; the launch traced here: 4990 us
  waiting for transfers between devices  2520 us (50%)
  local copies, waits for them, and re-layouts  886 us (18%)
  matrix products  629 us (13%)
  other arithmetic  539 us (11%)
  blocking collectives  385 us (8%)
    reduce_scatter x8, waiting for transfers between devices, project_forward(): summed = lax.psum_scatter(joined, 'col', scatter_dimension=1, tiled=True)  1490 us
    all_gather x4, waiting for transfers between devices, project_backward(): spread_out = lax.all_gather(grad_out[:, None, :], 'col', axis=1, tiled=True)  384 us
    psum x10, blocking collectives, feature_sums(): return lax.psum(stacked, ('row', 'col'))  380 us
    all_gather x8, waiting for transfers between devices, project_forward(): gathered = lax.all_gather(stack_in, 'row', axis=2, tiled=True)  339 us
    dynamic_update_slice x160, local copies, waits for them, and re-layouts, attention_mixing_complete(): lax.scan(step_fn, initial, (reshaped(acceptance_entries), reshaped(lookup...  282 us
    dot_general x160, matrix products, attention_mixing_segmented(): jnp.einsum('shi,shj->hij', end_k * tail_mask[:, None, None], payload_entr...  173 us
    dynamic_slice x256, local copies, waits for them, and re-layouts, attention_mixing_complete(): lax.scan(step_fn, initial, (reshaped(acceptance_entries), reshaped(lookup...  149 us
    mul x96, other arithmetic, attention_mixing_segmented(): jnp.sum(acceptance_entries * extra_current_coeffs[None] * lookup_sources,...  127 us
  transfers between devices with their start and end apart: 25, of which 25 were waited for; matrix products, arithmetic and copies ran while one was open for 2% of the time, Pallas kernels for 0%

commit v1 on v0

v1 whole, which is shorter than its diff:
```python
import functools

import jax
import jax.numpy as jnp
from jax import lax
from jax.experimental import pallas as pl
from jax.experimental.pallas import tpu as pltpu
from jax.sharding import Mesh, PartitionSpec as P

HEAD = 64
SEQ = 1024
NPAR = 14
CHUNK = 128
LANES = 128
F32 = jnp.float32
BF16 = jnp.bfloat16
norm_eps = 1e-05
group_eps = 0.00064
head_divisor = 8.0


NN = (((1,), (0,)), ((), ()))
NT = (((1,), (1,)), ((), ()))
TN = (((0,), (0,)), ((), ()))


def split(a):
    hi = a.astype(BF16)
    return hi, (a - hi.astype(F32)).astype(BF16)


def mm3(a, b, dims):
    (ah, al), (bh, bl) = a, b
    one = functools.partial(lax.dot_general, dimension_numbers=dims, preferred_element_type=F32)
    return one(ah, bh) + (one(ah, bl) + one(al, bh))


def rows_of(pair, h):
    return tuple(part[h * HEAD : (h + 1) * HEAD] for part in pair)


def per_head(value, heads):
    return value.reshape(heads, HEAD, value.shape[-1])


def decay_tables(tab_ref):
    lw = tab_ref[:, 0:1]
    tau = lax.broadcasted_iota(jnp.int32, (1, CHUNK), 1).astype(F32)
    mid = CHUNK // 2
    er = jnp.exp(lw * (tau - mid))
    ek = jnp.exp(-lw * (tau + 1.0 - mid))
    eend = jnp.exp(lw * (CHUNK - 1.0 - tau))
    ein = jnp.exp(lw * tau)
    return er, ek, eend, ein


def chunk_masks(ls_ref, base):
    ls = ls_ref[...]
    s_at = lax.broadcasted_iota(jnp.int32, (CHUNK, CHUNK), 0) + base
    t_at = lax.broadcasted_iota(jnp.int32, (CHUNK, CHUNK), 1) + base
    allowed = (s_at < t_at) & (s_at >= ls)
    opened = (ls < base).astype(F32)
    last = jnp.max(ls, axis=1, keepdims=True)
    tail = ((lax.broadcasted_iota(jnp.int32, (1, CHUNK), 1) + base) >= last).astype(F32)
    open_end = (last < base).astype(F32)
    return allowed, opened, tail, open_end


def diagonal_blocks(width):
    a = lax.broadcasted_iota(jnp.int32, (width, width), 0) // HEAD
    b = lax.broadcasted_iota(jnp.int32, (width, width), 1) // HEAD
    return a == b


def mix_forward_kernel(heads, r_ref, k_ref, v_ref, g_ref, tab_ref, row_ref, ls_ref,
                       z_ref, o_ref, st_ref, state):
    width = heads * HEAD
    base = pl.program_id(0) * CHUNK

    @pl.when(pl.program_id(0) == 0)
    def _():
        state[...] = jnp.zeros_like(state)

    st = state[...]
    st_ref[0] = st
    er, ek, eend, ein = decay_tables(tab_ref)
    allowed, opened, tail, open_end = chunk_masks(ls_ref, base)
    r, k, v = r_ref[...], k_ref[...], v_ref[...]
    rt, kt, vp = split(r * er), split(k * ek), split(v)
    outs = []
    for h in range(heads):
        scores = mm3(rows_of(kt, h), rows_of(rt, h), TN)
        scores = split(jnp.where(allowed, scores, 0.0))
        outs.append(mm3(rows_of(vp, h), scores, NN))
    o = jnp.concatenate(outs, axis=0)
    o = o + mm3(split(st), split(r * (ein * opened)), NN)
    ruk = jnp.sum(per_head(r * tab_ref[:, 1:2] * k, heads), axis=1, keepdims=True)
    o = o + (per_head(v, heads) * ruk).reshape(width, CHUNK)
    fresh = mm3(vp, split(k * (eend * tail)), NT)
    state[...] = st * (jnp.exp(row_ref[0:1, :] * CHUNK) * open_end) + jnp.where(
        diagonal_blocks(width), fresh, 0.0
    )
    o_ref[...] = o
    x = per_head(o / head_divisor, heads)
    center = jnp.mean(x, axis=1, keepdims=True)
    spread = jnp.mean(jnp.square(x - center), axis=1, keepdims=True)
    y = ((x - center) * lax.rsqrt(spread + group_eps)).reshape(width, CHUNK)
    g = g_ref[...]
    z_ref[...] = ((y * tab_ref[:, 2:3] + tab_ref[:, 3:4]) * (g * jax.nn.sigmoid(g))).astype(BF16)


def mix_backward_kernel(heads, r_ref, k_ref, v_ref, g_ref, o_ref, dz_ref, st_ref, tab_ref, row_ref,
                        ls_ref, dr_ref, dk_ref, dv_ref, dg_ref, acc_ref, row_acc_ref, dstate):
    width = heads * HEAD
    base = (pl.num_programs(0) - 1 - pl.program_id(0)) * CHUNK

    @pl.when(pl.program_id(0) == 0)
    def _():
        dstate[...] = jnp.zeros_like(dstate)
        acc_ref[...] = jnp.zeros_like(acc_ref)
        row_acc_ref[...] = jnp.zeros_like(row_acc_ref)

    u, gain, bias = tab_ref[:, 1:2], tab_ref[:, 2:3], tab_ref[:, 3:4]
    x = per_head(o_ref[...] / head_divisor, heads)
    center = jnp.mean(x, axis=1, keepdims=True)
    spread = jnp.mean(jnp.square(x - center), axis=1, keepdims=True)
    inverse = lax.rsqrt(spread + group_eps)
    xh = (x - center) * inverse
    xh_flat = xh.reshape(width, CHUNK)
    g, dz = g_ref[...], dz_ref[...]
    sg = jax.nn.sigmoid(g)
    dy = dz * (g * sg)
    dg_ref[...] = (dz * (xh_flat * gain + bias) * (sg * (1.0 + g * (1.0 - sg)))).astype(BF16)
    acc_ref[2] += dy * xh_flat
    acc_ref[3] += dy
    dxh = per_head(dy * gain, heads)
    dx = inverse * (
        dxh
        - jnp.mean(dxh, axis=1, keepdims=True)
        - xh * jnp.mean(dxh * xh, axis=1, keepdims=True)
    )
    do = dx.reshape(width, CHUNK) / head_divisor
    er, ek, eend, ein = decay_tables(tab_ref)
    allowed, opened, tail, open_end = chunk_masks(ls_ref, base)
    r, k, v = r_ref[...], k_ref[...], v_ref[...]
    st, dst = st_ref[0], dstate[...]
    rt, kt, vp, dop = split(r * er), split(k * ek), split(v), split(do)
    dst_p = split(dst)
    dr_in, dk_in, dv_in = [], [], []
    for h in range(heads):
        rt_h, kt_h, v_h, do_h = rows_of(rt, h), rows_of(kt, h), rows_of(vp, h), rows_of(dop, h)
        a = split(jnp.where(allowed, mm3(v_h, do_h, TN), 0.0))
        q = split(jnp.where(allowed, mm3(kt_h, rt_h, TN), 0.0))
        dr_in.append(mm3(kt_h, a, NN))
        dk_in.append(mm3(rt_h, a, NT))
        dv_in.append(mm3(do_h, q, NT))
    ein_open = ein * opened
    end_tail = eend * tail
    dr = jnp.concatenate(dr_in, axis=0) * er + mm3(split(st), dop, TN) * ein_open
    dk = jnp.concatenate(dk_in, axis=0) * ek + mm3(dst_p, vp, TN) * end_tail
    dv = jnp.concatenate(dv_in, axis=0) + mm3(dst_p, split(k * end_tail), NN)
    fresh = mm3(dop, split(r * ein_open), NT)
    dst_new = dst * (jnp.exp(row_ref[0:1, :] * CHUNK) * open_end) + jnp.where(
        diagonal_blocks(width), fresh, 0.0
    )
    dstate[...] = dst_new
    tau = lax.broadcasted_iota(jnp.int32, (1, CHUNK), 1).astype(F32)
    acc_ref[0] += tau * (r * dr) - (tau + 1.0) * (k * dk)
    row_acc_ref[0:1, :] += CHUNK * jnp.sum(st * dst_new, axis=0, keepdims=True)
    vd = jnp.sum(per_head(v * do, heads), axis=1, keepdims=True)
    vd = jnp.broadcast_to(vd, (heads, HEAD, CHUNK)).reshape(width, CHUNK)
    acc_ref[1] += r * k * vd
    ruk = jnp.sum(per_head(r * u * k, heads), axis=1, keepdims=True)
    dr_ref[...] = (dr + u * k * vd).astype(BF16)
    dk_ref[...] = (dk + u * r * vd).astype(BF16)
    dv_ref[...] = (dv + (per_head(do, heads) * ruk).reshape(width, CHUNK)).astype(BF16)


def time_forward(r, k, v, g, tab, row, ls):
    width, tokens = r.shape
    heads, chunks = width // HEAD, tokens // CHUNK
    piece = pl.BlockSpec((width, CHUNK), lambda c: (0, c))
    return pl.pallas_call(
        functools.partial(mix_forward_kernel, heads),
        grid=(chunks,),
        in_specs=[piece] * 4 + [
            pl.BlockSpec(tab.shape, lambda c: (0, 0)),
            pl.BlockSpec(row.shape, lambda c: (0, 0)),
            pl.BlockSpec((1, CHUNK), lambda c: (0, c)),
        ],
        out_specs=[piece, piece, pl.BlockSpec((1, width, width), lambda c: (c, 0, 0))],
        out_shape=[
            jax.ShapeDtypeStruct((width, tokens), BF16),
            jax.ShapeDtypeStruct((width, tokens), F32),
            jax.ShapeDtypeStruct((chunks, width, width), F32),
        ],
        scratch_shapes=[pltpu.VMEM((width, width), F32)],
        compiler_params=pltpu.CompilerParams(vmem_limit_bytes=48 << 20),
        name="time_forward",
    )(r, k, v, g, tab, row, ls)


def time_backward(r, k, v, g, o, dz, states, tab, row, ls):
    width, tokens = r.shape
    heads, chunks = width // HEAD, tokens // CHUNK
    piece = pl.BlockSpec((width, CHUNK), lambda c: (0, chunks - 1 - c))
    return pl.pallas_call(
        functools.partial(mix_backward_kernel, heads),
        grid=(chunks,),
        in_specs=[piece] * 6 + [
            pl.BlockSpec((1, width, width), lambda c: (chunks - 1 - c, 0, 0)),
            pl.BlockSpec(tab.shape, lambda c: (0, 0)),
            pl.BlockSpec(row.shape, lambda c: (0, 0)),
            pl.BlockSpec((1, CHUNK), lambda c: (0, chunks - 1 - c)),
        ],
        out_specs=[piece] * 4 + [
            pl.BlockSpec((4, width, CHUNK), lambda c: (0, 0, 0)),
            pl.BlockSpec((8, width), lambda c: (0, 0)),
        ],
        out_shape=[jax.ShapeDtypeStruct((width, tokens), BF16)] * 4 + [
            jax.ShapeDtypeStruct((4, width, CHUNK), F32),
            jax.ShapeDtypeStruct((8, width), F32),
        ],
        scratch_shapes=[pltpu.VMEM((width, width), F32)],
        compiler_params=pltpu.CompilerParams(vmem_limit_bytes=48 << 20),
        name="time_backward",
    )(r, k, v, g, o, dz, states, tab, row, ls)


class Moves:
    def __init__(self, sizes):
        self.sizes = sizes
        self.nz = sizes["col"]
        self.x = lax.axis_index("seq")
        self.core = lax.axis_index("core")
        self.z = lax.axis_index("col")

    def shift(self, v, axis, k):
        n = self.sizes[axis]
        return lax.ppermute(v, axis, [(i, (i + k) % n) for i in range(n)])

    def swap(self, v):
        return self.shift(v, "core", 1)

    def cross(self, v):
        return self.shift(v, "seq", 1)

    def hop(self, v, k):
        return self.shift(v, "col", k)

    def ordered(self, at, mine, other, axis):
        return jnp.where(
            at == 0,
            jnp.concatenate([mine, other], axis=axis),
            jnp.concatenate([other, mine], axis=axis),
        )

    def pick(self, v, at):
        return lax.dynamic_index_in_dim(v, at, 0, keepdims=False)

    def gather(self, v):
        half = v.shape[0] // 2
        up, down = [v[:half]], [v[half:]]
        for _ in range(1, self.nz):
            up.append(self.hop(up[-1], 1))
            down.append(self.hop(down[-1], -1))
        rows = []
        for k in range(self.nz):
            a, b = up[k], down[(self.nz - k) % self.nz]
            rows += [a, b, self.swap(a), self.swap(b)]
        return jnp.concatenate(rows, axis=0)

    def scatter_sum(self, p):
        half = p.shape[0] // (self.nz * 4)
        q = p.reshape(self.nz, 2, 2, half, p.shape[1])
        s = [q[k, 0] + self.swap(q[k, 1].astype(BF16)).astype(F32) for k in range(self.nz)]
        low = s[self.nz - 1][0]
        for k in range(self.nz - 2, -1, -1):
            low = self.hop(low.astype(BF16), -1).astype(F32) + s[k][0]
        high = s[1][1]
        for k in range(2, self.nz + 1):
            high = self.hop(high.astype(BF16), 1).astype(F32) + s[k % self.nz][1]
        return jnp.concatenate([low, high], axis=0)

    def small_sum(self, v):
        v = v + self.swap(v)
        total = v
        for k in range(1, self.nz):
            total = total + self.hop(v, k)
        return total

    def over_dp(self, v):
        total = v.astype(F32)
        for k in range(1, self.sizes["dp"]):
            total = total + self.shift(v, "dp", k).astype(F32)
        return total

    def columns(self, stacked):
        nz = self.nz
        mine, other = [], []
        for k in range(nz):
            piece = self.pick(stacked, (self.z + k) % nz)
            piece = self.hop(piece, k) if k else piece
            mine.append(piece)
            other.append(self.cross(piece))
        return jnp.stack(mine), jnp.stack(other)

    def columns_of(self, pair, start, rows):
        mine, other = (v[:, start : start + rows][None] for v in pair)
        v = self.ordered(self.x, mine, other, 0)
        v = v.reshape(2, self.nz, rows, 2, 2, -1)
        v = jnp.where(self.core == 0, v, v[:, :, :, :, ::-1])
        return v.transpose(0, 2, 1, 4, 3, 5).reshape(2 * rows, -1)

    def lines(self, a):
        nz, rows, width = a.shape
        v = a.reshape(nz, rows, 2, 2, width // 4)
        even, odd = v[:, :, :, 0], v[:, :, :, 1]
        keep = jnp.where(self.core == 0, even, odd)
        send = jnp.where(self.core == 0, odd, even)
        both = jnp.stack([keep, self.swap(send)]).reshape(2, nz, rows, width // 2)
        both = self.ordered(self.x, both[None], self.cross(both)[None], 0)
        both = both.transpose(2, 1, 0, 3, 4)
        order = [self.pick(both, (self.z - k) % nz) for k in range(nz)]
        return jnp.stack(order).reshape(nz * 4 * rows, width // 2)

    def return_columns(self, grad):
        nz = self.nz
        rows = grad.shape[0] // 2
        v = grad.reshape(2, rows, nz, 2, 2, -1)
        sent = self.cross(self.pick(v, 1 - self.x).astype(BF16))
        v = self.pick(v, self.x) + sent.astype(F32)
        v = jnp.where(self.core == 0, v, v[:, :, ::-1])
        v = v.transpose(1, 0, 3, 2, 4).reshape(nz, rows, -1).astype(BF16)
        got = [self.hop(v[k], -k) if k else v[k] for k in range(nz)]
        got = jnp.stack([self.over_dp(piece) for piece in got])
        return jnp.stack([self.pick(got, (c - self.z) % nz) for c in range(nz)])

    def return_lines(self, grad):
        nz = self.nz
        rows = grad.shape[0] // (4 * nz)
        v = grad.reshape(nz * 2, 2, rows, -1)
        v = v.transpose(1, 0, 2, 3)
        sent = self.cross(self.pick(v, 1 - self.x).astype(BF16))
        v = (self.pick(v, self.x) + sent.astype(F32)).reshape(nz, 2, rows, 2, 1, -1).astype(BF16)
        v = self.ordered(self.core, v[:, 0], self.swap(v[:, 1]), 3)
        v = self.over_dp(v.reshape(nz, rows, -1))
        return jnp.stack([self.pick(v, (self.z - c) % nz) for c in range(nz)])

    def to_storage(self, v):
        v = v.reshape(2, v.shape[0] // 2, v.shape[1])
        return self.ordered(self.x, self.pick(v, self.x), self.cross(self.pick(v, 1 - self.x)), 1)


def previous(v, keep):
    return jnp.concatenate([jnp.zeros_like(v[:, :1]), v[:, :-1]], axis=1) * keep


def following(v, keep):
    return jnp.concatenate([v[:, 1:] * keep[:, 1:], jnp.zeros_like(v[:, :1])], axis=1)


def norm_stats(v):
    center = jnp.mean(v, axis=0, keepdims=True)
    spread = jnp.mean(jnp.square(v - center), axis=0, keepdims=True)
    return center, lax.rsqrt(spread + norm_eps)


def forward_dot(weight, v):
    return jnp.einsum("oi,it->ot", weight, v, preferred_element_type=F32)


def back_dot(weight, grad):
    return jnp.einsum("oi,ot->it", weight, grad, preferred_element_type=F32)


def weight_dot(grad, v):
    return jnp.einsum("ot,it->oi", grad, v, preferred_element_type=F32)


def mixing_back(grads, coeffs, normed, keep):
    difference = normed - previous(normed, keep)
    straight, shifted, sums = 0.0, 0.0, []
    for grad, coeff in zip(grads, coeffs):
        scaled = grad * coeff
        straight = straight + scaled
        shifted = shifted + (grad - scaled)
        sums.append(jnp.sum(grad * difference, axis=1, keepdims=True))
    return straight + following(shifted, keep), sums


def norm_back_sums(grad, gain, unit):
    scaled = grad * gain
    return jnp.concatenate(
        [jnp.sum(scaled, axis=0, keepdims=True), jnp.sum(scaled * unit, axis=0, keepdims=True)], axis=0
    )


def with_columns(v, columns):
    pad = jnp.zeros((v.shape[0], LANES - len(columns)), v.dtype)
    return jnp.concatenate([v] + list(columns) + [pad], axis=1)


def shards(sizes, tokens, segments, channel_table, w_recept, w_key, w_value, w_gate, w_output,
           ffn_key, ffn_value, ffn_recept, cotangent):
    m = Moves(sizes)
    x = m.x
    count = tokens.shape[1] // 2
    features = tokens.shape[0] * 4 * m.nz

    def mine_of(v, at):
        return lax.dynamic_slice_in_dim(v, at * count, count, axis=v.ndim - 1)

    positions = jnp.arange(segments.shape[0], dtype=jnp.int32)
    earlier = jnp.concatenate([segments[:1], segments[:-1]])
    starts = (positions % SEQ == 0) | (segments != earlier)
    starts = mine_of(starts[None].astype(jnp.int32), x)
    keep = (1 - starts).astype(F32)
    at = jnp.arange(count, dtype=jnp.int32)
    last_start = jnp.max(
        jnp.where((starts > 0) & (at[None, :] <= at[:, None]), at[None, :], 0), axis=1
    )[None]

    table_t = channel_table.T
    table_t = jnp.concatenate(
        [table_t, jnp.zeros((table_t.shape[0], LANES - NPAR), BF16)], axis=1
    )
    here = jnp.concatenate([mine_of(tokens, x), table_t, mine_of(cotangent, x)], axis=1)
    there = jnp.concatenate([mine_of(tokens, 1 - x), table_t, mine_of(cotangent, 1 - x)], axis=1)
    own = m.ordered(x, here, m.cross(there), 0)
    gathered = m.gather(own[:, : count + LANES])
    tok_own = own[:, :count].astype(F32)
    tab_own = own[:, count : count + NPAR].astype(F32)
    cot_own = own[:, count + LANES :].astype(F32)
    all_tokens = gathered[:, :count].astype(F32)
    tab = gathered[:, count : count + NPAR].astype(F32)

    def own_col(n):
        return tab_own[:, n : n + 1]

    def col(n):
        return tab[:, n : n + 1]

    rows = w_recept.shape[1]
    first = m.columns(jnp.concatenate([w_recept, w_key, w_value, w_gate], axis=1))
    w_first = [m.columns_of(first, n * rows, rows) for n in range(4)]

    center_one, inverse_one = norm_stats(all_tokens)
    normed_one = (all_tokens - center_one) * inverse_one * col(0) + col(1)
    shifted_one = previous(normed_one, keep)
    mixes = [
        (normed_one * col(2 + n) + shifted_one * (1.0 - col(2 + n))).astype(BF16) for n in range(4)
    ]
    r, k, v, g = [forward_dot(w_first[n], mixes[n]) for n in range(4)]

    lw = -jnp.exp(own_col(6))
    kernel_tab = jnp.concatenate([lw, own_col(7), own_col(8), own_col(9)], axis=1)
    kernel_row = jnp.broadcast_to(lw.T, (8, lw.shape[0]))
    z, o, states = time_forward(r, k, v, g, kernel_tab, kernel_row, last_start)

    w_out = m.lines(w_output)
    branch = m.scatter_sum(forward_dot(w_out, z))
    h = tok_own + branch
    all_h = m.gather(h.astype(BF16)).astype(F32)

    hidden = ffn_key.shape[1]
    second = m.columns(jnp.concatenate([ffn_recept, ffn_key], axis=1))
    w_rec = m.columns_of(second, 0, rows)
    w_key_ffn = m.columns_of(second, rows, hidden)
    w_val = m.lines(ffn_value)

    center_two, inverse_two = norm_stats(all_h)
    normed_two = (all_h - center_two) * inverse_two * col(10) + col(11)
    shifted_two = previous(normed_two, keep)
    e_k, e_r = [
        (normed_two * col(n) + shifted_two * (1.0 - col(n))).astype(BF16) for n in (12, 13)
    ]
    rr = forward_dot(w_rec, e_r)
    gate = jax.nn.sigmoid(rr)
    dvv = (cot_own * gate).astype(BF16)
    all_dvv = m.gather(dvv)
    kk = jax.nn.relu(forward_dot(w_key_ffn, e_k))
    act = jnp.square(kk).astype(BF16)
    vv = m.scatter_sum(forward_dot(w_val, act))
    mixed = (h + gate * vv).astype(BF16)
    drr = (cot_own * vv * gate * (1.0 - gate)).astype(BF16)

    grad_value = m.return_lines(weight_dot(all_dvv, act))
    dkk = (back_dot(w_val, all_dvv) * 2.0 * kk).astype(BF16)
    grad_key = m.return_columns(weight_dot(dkk, e_k))
    grad_rec = m.return_columns(weight_dot(drr, e_r))
    dn_two, sums_two = mixing_back(
        [back_dot(w_key_ffn, dkk), back_dot(w_rec, drr)], [col(12), col(13)], normed_two, keep
    )
    unit_all_two = (all_h - center_two) * inverse_two
    totals_two = m.small_sum(norm_back_sums(dn_two, col(10), unit_all_two)) / features
    summed_two = m.scatter_sum(with_columns(dn_two, sums_two))
    dn_two_own = summed_two[:, :count]
    unit_two = (h - center_two) * inverse_two
    gain_two = jnp.sum(dn_two_own * unit_two, axis=1, keepdims=True)
    bias_two = jnp.sum(dn_two_own, axis=1, keepdims=True)
    dh = cot_own + inverse_two * (
        dn_two_own * own_col(10) - totals_two[0:1] - unit_two * totals_two[1:2]
    )

    all_dh = m.gather(dh.astype(BF16))
    dz = back_dot(w_out, all_dh)
    grad_output = m.return_lines(weight_dot(all_dh, z))
    *dps, acc, row_acc = time_backward(
        r, k, v, g, o, dz, states, kernel_tab, kernel_row, last_start
    )
    acc = jnp.sum(acc, axis=2)
    grad_rows = [
        ((acc[0] + row_acc[0]) * lw[:, 0])[:, None],
        acc[1][:, None],
        acc[2][:, None],
        acc[3][:, None],
    ]
    grads_time = [m.return_columns(weight_dot(dps[n], mixes[n])) for n in range(4)]
    dn_one, sums_one = mixing_back(
        [back_dot(w_first[n], dps[n]) for n in range(4)],
        [col(2 + n) for n in range(4)],
        normed_one,
        keep,
    )
    unit_all_one = (all_tokens - center_one) * inverse_one
    totals_one = m.small_sum(norm_back_sums(dn_one, col(0), unit_all_one)) / features
    summed_one = m.scatter_sum(with_columns(dn_one, sums_one))
    dn_one_own = summed_one[:, :count]
    unit_one = (tok_own - center_one) * inverse_one
    gain_one = jnp.sum(dn_one_own * unit_one, axis=1, keepdims=True)
    bias_one = jnp.sum(dn_one_own, axis=1, keepdims=True)
    grad_tokens = dh + inverse_one * (
        dn_one_own * own_col(0) - totals_one[0:1] - unit_one * totals_one[1:2]
    )

    sums = with_columns(
        gain_one,
        [bias_one, summed_one[:, count : count + 4]]
        + grad_rows
        + [gain_two, bias_two, summed_two[:, count : count + 2]],
    )[:, :NPAR]
    sums = sums.reshape(2, sums.shape[0] // 2, NPAR)
    table = m.pick(sums, x) + m.cross(m.pick(sums, 1 - x))
    table = m.over_dp(table).T
    return (
        m.to_storage(mixed),
        m.to_storage(grad_tokens),
        table,
        grads_time[0],
        grads_time[1],
        grads_time[2],
        grads_time[3],
        grad_output,
        grad_key,
        grad_value,
        grad_rec,
    )


def solution(mesh):
    sizes = {"dp": mesh.shape["dp"], "seq": 2, "core": mesh.shape["row"] // 2, "col": mesh.shape["col"]}
    fine = Mesh(mesh.devices.reshape(tuple(sizes.values())), tuple(sizes))
    both = P(("col", "seq", "core"), "dp")
    weight = P(None, ("seq", "core"), "col")
    table = P(None, ("col", "seq", "core"))
    return jax.shard_map(
        functools.partial(shards, sizes),
        mesh=fine,
        in_specs=(both, P("dp"), table) + (weight,) * 8 + (both,),
        out_specs=(both, both, table) + (weight,) * 8,
        check_vma=False,
    )
```

time: 5030 us -> 1230 us (0.24)
  waiting for transfers between devices: 2520 us -> 250 us
  local copies, waits for them, and re-layouts: 886 us -> 291 us
  matrix products: 629 us -> 107 us
  blocking collectives: 385 us -> 0 us
  other arithmetic: 539 us -> 308 us
  starting transfers between devices: 2.19 us -> 233 us
    reduce_scatter x10 -> x0, waiting for transfers between devices: 1570 us -> none  [the longest x8 1490 us: project_forward(): summed = lax.psum_scatter(joined, 'col', scatter_dimension=1, tiled=True)]
    all_gather x12 -> x0, waiting for transfers between devices: 722 us -> none  [the longest x4 384 us: project_backward(): spread_out = lax.all_gather(grad_out[:, None, :], 'col', axis=1, tiled=True)]
    dot_general x704 -> x24, matrix products: 629 us -> 107 us  [the longest x8 52.4 us: back_dot(): return jnp.einsum('oi,ot->it', weight, grad, preferred_element_type=F32)]
    psum x11 -> x0, blocking collectives: 385 us -> none  [the longest x10 380 us: feature_sums(): return lax.psum(stacked, ('row', 'col'))]
    dynamic_update_slice x160 -> x0, local copies, waits for them, and re-layouts: 282 us -> none  [attention_mixing_complete(): lax.scan(step_fn, initial, (reshaped(acceptance_entries), reshaped(lookup...]
    ppermute x0 -> x181, waiting for transfers between devices: none -> 250 us  [shift(): return lax.ppermute(v, axis, [(i, (i + k) % n) for i in range(n)])]
    ppermute x0 -> x181, starting transfers between devices: none -> 233 us  [shift(): return lax.ppermute(v, axis, [(i, (i + k) % n) for i in range(n)])]
    dynamic_slice x256 -> x14, local copies, waits for them, and re-layouts: 149 us -> 6.46 us  [the longest x13 5.17 us: pick(): return lax.dynamic_index_in_dim(v, at, 0, keepdims=False)]
  transfers between devices with their start and end apart: 25 -> 181, of which waited for: 25 -> 68; matrix products, arithmetic and copies ran while one was open for 2% -> 42% of each run, Pallas kernels for 0% -> 1%
where the time goes in v1:
time: 1230 us; the launch traced here: 1220 us
  other arithmetic  308 us (25%)
  local copies, waits for them, and re-layouts  291 us (24%)
  waiting for transfers between devices  250 us (20%)
  starting transfers between devices  233 us (19%)
  matrix products  107 us (9%)
  Pallas kernels  26.2 us (2%)
    ppermute x181, waiting for transfers between devices, shift(): return lax.ppermute(v, axis, [(i, (i + k) % n) for i in range(n)])  250 us
    ppermute x181, starting transfers between devices, shift(): return lax.ppermute(v, axis, [(i, (i + k) % n) for i in range(n)])  233 us
    unnamed x394, local copies, waits for them, and re-layouts  69 us
    reduce_sum x2, other arithmetic, norm_back_sums(): jnp.sum(scaled, axis=0, keepdims=True)  54.2 us
    dot_general x8, matrix products, back_dot(): return jnp.einsum('oi,ot->it', weight, grad, preferred_element_type=F32)  52.4 us
    mul x2, other arithmetic, following(): v[:, 1:] * keep[:, 1:]  47.5 us
    concatenate x24, local copies, waits for them, and re-layouts, ordered(): jnp.concatenate([mine, other], axis=axis)  42.7 us
    concatenate x11, local copies, waits for them, and re-layouts, with_columns(): return jnp.concatenate([v] + list(columns) + [pad], axis=1)  33.1 us
  transfers between devices with their start and end apart: 181, of which 68 were waited for; matrix products, arithmetic and copies ran while one was open for 42% of the time, Pallas kernels for 1%

profile of v1, /device:TPU:0, one launch (start us, length us, event | category | flops | bytes accessed | tf_op | source)
XLA Modules:
  0.0 1219.3 jit_solution(748211134378381632)
XLA Ops:
  28.6 20.8 %collective-permute-start.34 = (bf16[576,512]{1,0:T(8,128)(2,1)}, bf16[576,512]{1,0:T(8,128)(2,1)S(1)}, u32[]{:S(2)}, u32[]{:S(2)}) collective-permute-start(bf16[576,512]{1,0:T(8,128)(2,1)} %get-tuple-element.178), channel_id=1, source_target_pairs={{0,1},{1,2},{2,3},{3,0},{4,5},{5,6},{6,7},{7,4},{8,9},{9,10},{10,1... | collective-permute-start | bytes 1769480 | tf_op jit(solution)/shard_map/ppermute | solution.py:240
  51.8 31.1 %collective-permute-start.36 = (bf16[576,512]{1,0:T(8,128)(2,1)}, bf16[576,512]{1,0:T(8,128)(2,1)}, u32[]{:S(2)}, u32[]{:S(2)}) collective-permute-start(bf16[576,512]{1,0:T(8,128)(2,1)} %get-tuple-element.176), channel_id=1, source_target_pairs={{0,3},{1,0},{2,1},{3,2},{4,7},{5,4},{6,5},{7,6},{8,11},{9,8},{10,9... | collective-permute-start | bytes 1769480 | tf_op jit(solution)/shard_map/ppermute | solution.py:240
  115.0 7.0 collective-permute-start.12
  125.4 4.9 collective-permute-done.12
  148.1 5.6 broadcast_select_fusion.4
  172.2 7.0 collective-permute-start.18
  185.4 7.1 collective-permute-done.14
  202.3 6.6 broadcast_select_fusion.2
  237.3 6.8 slice_reduce_fusion.4
  247.8 10.8 add_convert_fusion.2
  264.6 6.7 add_convert_fusion.5
  273.3 8.6 time_forward.1
  281.9 4.5 fusion.172
  295.7 4.8 fusion.69
  343.7 5.4 broadcast_select_fusion
  355.7 5.6 fusion.24
  361.3 7.2 reshape.471
  391.0 5.5 collective-permute-done.46
  397.2 4.6 collective-permute-done.52
  407.4 9.0 add_convert_fusion
  416.3 5.8 fusion.178
  422.2 6.7 fusion.173
  442.1 9.1 collective-permute-done.58
  476.4 4.3 collective-permute-done.62
  488.4 4.0 reshape.483
  500.4 8.4 broadcast_multiply_fusion.1
  525.4 4.4 collective-permute-done.175
  537.9 4.6 collective-permute-done.179
  544.2 4.3 collective-permute-done.180
  549.5 10.7 collective-permute-done.73
  564.1 4.3 multiply_convert_fusion
  568.4 6.5 fusion.185
  574.9 8.3 broadcast_multiply_fusion
  583.2 10.7 reshape.481
  593.9 17.2 %fusion.19 = f32[2048,1023]{1,0:T(8,128)} fusion(f32[2048,1024]{1,0:T(8,128)} %get-tuple-element.301, f32[2048,1024]{1,0:T(8,128)} %get-tuple-element.302, f32[2048,1024]{1,0:T(8,128)} %get-tuple-element.303, f32[2048,1024]{1,0:T(8,128)} %get-tuple-element.304, f32[1023]{0:T(1024)S(1)} %bitcast.595), kind=kLoop, calls=%fused_computation.28 | loop fusion | flops 8380416 | bytes 41906172 | tf_op jit(solution)/shard_map/mul | solution.py:360
  611.1 21.2 %multiply_reduce_fusion.7 = (f32[1024]{0:T(1024)S(1)}, f32[1024]{0:T(1024)S(1)}, f32[2048]{0:T(1024)S(1)}, f32[2048]{0:T(1024)S(1)}, f32[2048,1024]{1,0:T(8,128)}) fusion(f32[2048]{0:T(1024)S(1)} %get-tuple-element.102, f32[1024]{0:T(1024)S(1)} %add_rsqrt_fusion, f32[1024]{0:T(1024)S(1)} %broadcast_multiply_fusion.6, bf16[2048,1024]{1,0:T(8,128)(2,1)S(1)} %copy-done.17, ...), kind=kLoop, calls=%fused_computation.47 | loop fusion | flops 35645440 | bytes 62951424 | tf_op jit(solution)/shard_map/reduce_sum | solution.py:395
  635.1 11.8 concatenate.284
  647.0 4.4 convert.54
  653.5 7.0 fusion.125
  663.2 4.5 fusion.26
  670.9 5.8 collective-permute-done.89
  687.7 7.2 collective-permute-done.85
  699.0 7.6 collective-permute-done.91
  715.9 5.0 copy.364
  732.4 4.5 bitcast_add_fusion.1
  743.1 23.0 %collective-permute-done.170 = bf16[8,128,896]{1,2,0:T(8,128)(2,1)S(1)} collective-permute-done((bf16[8,128,896]{1,2,0:T(8,128)(2,1)}, bf16[8,128,896]{1,2,0:T(8,128)(2,1)S(1)}, u32[]{:S(2)}, u32[]{:S(2)}) %collective-permute-start.170) | collective-permute-done | bytes 1835040 | tf_op jit(solution)/shard_map/ppermute | solution.py:240
  805.8 17.6 %time_backward.1 = (bf16[256,1024]{1,0:T(8,128)(2,1)S(1)}, bf16[256,1024]{1,0:T(8,128)(2,1)S(1)}, bf16[256,1024]{1,0:T(8,128)(2,1)S(1)}, bf16[256,1024]{1,0:T(8,...) custom-call(f32[256,1024]{1,0:T(8,128)S(1)} %copy-done.6, f32[256,1024]{1,0:T(8,128)S(1)} %copy-done.4, ...), custom_call_target="tpu_custom_call" | custom-call | tf_op jit(solution)/shard_map/time_backward/pallas_call | solution.py:207
  826.0 7.4 broadcast_multiply_fusion.2
  836.1 7.3 broadcast_multiply_fusion.4
  846.0 7.2 broadcast_multiply_fusion.3
  855.9 7.3 broadcast_multiply_fusion.5
  880.8 30.3 %fusion.15 = f32[2048,1023]{1,0:T(8,128)} fusion(f32[2048,1024]{1,0:T(8,128)} %get-tuple-element.305, f32[2048,1024]{1,0:T(8,128)} %get-tuple-element.306, f32[2048,1024]{1,0:T(8,128)} %get-tuple-element.307, f32[2048,1024]{1,0:T(8,128)} %get-tuple-element.308, f32[2048,1024]{1,0:T(8,128)} %get-tuple-element.309, f32[2048,1024]{1,0:T(8,128)} %get-tuple-element.310, ...), kind=kLoop, calls=%fused_computation.20 | loop fusion | flops 16760832 | bytes 75427840 | tf_op jit(solution)/shard_map/mul | solution.py:360
  911.1 33.0 %multiply_reduce_fusion.6 = (f32[1024]{0:T(1024)S(1)}, f32[1024]{0:T(1024)S(1)}, f32[2048]{0:T(1024)S(1)}, f32[2048]{0:T(1024)S(1)}, f32[2048]{0:T(1024)S(1)}, /*index=5*/f32[2048]{0:T(1024)S(1)}, f32[2048,1024]{1,0:T(8,128)}) fusion(f32[2048]{0:T(1024)S(1)} %copy-done.122, f32[1024]{0:T(1024)S(1)} %copy-done.126, f32[1024]{0:T(1024)S(1)} %copy-done.118, ...), kind=kLoop, calls=%fused_computation.46 | loop fusion | flops 48224256 | bytes 96522240 | tf_op jit(solution)/shard_map/reduce_sum | solution.py:395
  950.6 12.6 %concatenate.294 = f32[4,2,2,128,1152]{4,3,2,1,0:T(8,128)} concatenate(f32[4,2,2,128,1024]{4,3,2,1,0:T(8,128)} %bitcast.549, f32[4,2,2,128,1]{4,3,2,1,0:T(8,128)} %copy.332, f32[4,2,2,128,1]{4,3,2,1,0:T(8,128)} %copy.333, f32[4,2,2,128,1]{4,3,2,1,0:T(8,128)} %copy.334, f32[4,2,2,128,1]{4,3,2,1,0:T(8,128)} %copy.335, f32[4,2,2,128,124]{4,3,2,1,0:T(8,128)} %broadcast_in_dim.44), dimensions={4} | concatenate | bytes 18874368 | tf_op jit(solution)/shard_map/concatenate | solution.py:401
  963.2 4.4 convert.57
  997.5 8.1 collective-permute-done.167
  1007.4 6.8 collective-permute-done.169
  1026.4 7.9 collective-permute-done.135
  1035.5 8.0 collective-permute-done.127
  1070.8 4.4 fusion.34
  1076.7 9.8 collective-permute-done.152
  1088.6 4.2 collective-permute-done.144
  1094.0 4.3 collective-permute-done.136
  1213.9 5.1 copy.371
  (1049 shorter events, 648.2 us)
Async XLA Ops:
  3.8 90.4 %collective-permute-start = (bf16[128,2176]{1,0:T(8,128)(2,1)}, bf16[128,2176]{1,0:T(8,128)(2,1)}, u32[]{:S(2)}, u32[]{:S(2)}) collective-permute-start(bf16[128,2176]{1,0:T(8,128)(2,1)} %concatenate.236), channel_id=1, source_target_pairs={{0,8},{8,0},{1,9},{9,1},{2,10},{10,2},{3,11},{11,3},{4,12},{12,4},... | collective-permute-start | bytes 1671176 | tf_op jit(solution)/shard_map/ppermute | solution.py:240
  13.1 38.0 %collective-permute-start.4 = (bf16[512,512]{1,0:T(8,128)(2,1)}, bf16[512,512]{1,0:T(8,128)(2,1)}, u32[]{:S(2)}, u32[]{:S(2)}) collective-permute-start(bf16[512,512]{1,0:T(8,128)(2,1)} %get-tuple-element.189), channel_id=1, source_target_pairs={{0,2},{1,3},{2,0},{3,1},{4,6},{5,7},{6,4},{7,5},{8,10},{9,11},{10,... | collective-permute-start | bytes 1572872 | tf_op jit(solution)/shard_map/ppermute | solution.py:240
  15.7 36.1 %collective-permute-start.5 = (bf16[512,512]{1,0:T(8,128)(2,1)}, bf16[512,512]{1,0:T(8,128)(2,1)}, u32[]{:S(2)}, u32[]{:S(2)}) collective-permute-start(bf16[512,512]{1,0:T(8,128)(2,1)} %get-tuple-element.188), channel_id=1, source_target_pairs={{0,3},{1,0},{2,1},{3,2},{4,7},{5,4},{6,5},{7,6},{8,11},{9,8},{10,9... | collective-permute-start | bytes 1572872 | tf_op jit(solution)/shard_map/ppermute | solution.py:240
  24.7 106.9 %collective-permute-start.6 = (bf16[512,512]{1,0:T(8,128)(2,1)}, bf16[512,512]{1,0:T(8,128)(2,1)}, u32[]{:S(2)}, u32[]{:S(2)}) collective-permute-start(bf16[512,512]{1,0:T(8,128)(2,1)} %bitcast.13), channel_id=1, source_target_pairs={{0,8},{8,0},{1,9},{9,1},{2,10},{10,2},{3,11},{11,3},{4,12},{12,4},... | collective-permute-start | bytes 1572872 | tf_op jit(solution)/shard_map/ppermute | solution.py:240
  28.6 71.0 %collective-permute-start.34 = (bf16[576,512]{1,0:T(8,128)(2,1)}, bf16[576,512]{1,0:T(8,128)(2,1)S(1)}, u32[]{:S(2)}, u32[]{:S(2)}) collective-permute-start(bf16[576,512]{1,0:T(8,128)(2,1)} %get-tuple-element.178), channel_id=1, source_target_pairs={{0,1},{1,2},{2,3},{3,0},{4,5},{5,6},{6,7},{7,4},{8,9},{9,10},{10,1... | collective-permute-start | bytes 1769480 | tf_op jit(solution)/shard_map/ppermute | solution.py:240
  51.1 50.1 %collective-permute-start.35 = (bf16[576,512]{1,0:T(8,128)(2,1)}, bf16[576,512]{1,0:T(8,128)(2,1)S(1)}, u32[]{:S(2)}, u32[]{:S(2)}) collective-permute-start(bf16[576,512]{1,0:T(8,128)(2,1)} %get-tuple-element.177), channel_id=1, source_target_pairs={{0,2},{1,3},{2,0},{3,1},{4,6},{5,7},{6,4},{7,5},{8,10},{9,11},{10,... | collective-permute-start | bytes 1769480 | tf_op jit(solution)/shard_map/ppermute | solution.py:240
  51.8 53.3 %collective-permute-start.36 = (bf16[576,512]{1,0:T(8,128)(2,1)}, bf16[576,512]{1,0:T(8,128)(2,1)}, u32[]{:S(2)}, u32[]{:S(2)}) collective-permute-start(bf16[576,512]{1,0:T(8,128)(2,1)} %get-tuple-element.176), channel_id=1, source_target_pairs={{0,3},{1,0},{2,1},{3,2},{4,7},{5,4},{6,5},{7,6},{8,11},{9,8},{10,9... | collective-permute-start | bytes 1769480 | tf_op jit(solution)/shard_map/ppermute | solution.py:240
  99.7 33.8 %collective-permute-start.7 = (bf16[512,512]{1,0:T(8,128)(2,1)}, bf16[512,512]{1,0:T(8,128)(2,1)}, u32[]{:S(2)}, u32[]{:S(2)}) collective-permute-start(bf16[512,512]{1,0:T(8,128)(2,1)} %collective-permute-done.3), channel_id=1, source_target_pairs={{0,8},{8,0},{1,9},{9,1},{2,10},{10,2},{3,11},{11,3},{4,12},{12,4},... | collective-permute-start | bytes 1572872 | tf_op jit(solution)/shard_map/ppermute | solution.py:240
  111.0 24.0 %collective-permute-start.8 = (bf16[512,512]{1,0:T(8,128)(2,1)}, bf16[512,512]{1,0:T(8,128)(2,1)S(1)}, u32[]{:S(2)}, u32[]{:S(2)}) collective-permute-start(bf16[512,512]{1,0:T(8,128)(2,1)} %collective-permute-done.4), channel_id=1, source_target_pairs={{0,8},{8,0},{1,9},{9,1},{2,10},{10,2},{3,11},{11,3},{4,12},{12,4},... | collective-permute-start | bytes 1572872 | tf_op jit(solution)/shard_map/ppermute | solution.py:240
  113.5 23.7 %collective-permute-start.9 = (bf16[512,512]{1,0:T(8,128)(2,1)}, bf16[512,512]{1,0:T(8,128)(2,1)S(1)}, u32[]{:S(2)}, u32[]{:S(2)}) collective-permute-start(bf16[512,512]{1,0:T(8,128)(2,1)} %collective-permute-done.5), channel_id=1, source_target_pairs={{0,8},{8,0},{1,9},{9,1},{2,10},{10,2},{3,11},{11,3},{4,12},{12,4},... | collective-permute-start | bytes 1572872 | tf_op jit(solution)/shard_map/ppermute | solution.py:240
  130.3 41.9 %collective-permute-start.37 = (bf16[576,512]{1,0:T(8,128)(2,1)S(1)}, bf16[576,512]{1,0:T(8,128)(2,1)}, u32[]{:S(2)}, u32[]{:S(2)}) collective-permute-start(bf16[576,512]{1,0:T(8,128)(2,1)S(1)} %bitcast.554), channel_id=1, source_target_pairs={{0,8},{8,0},{1,9},{9,1},{2,10},{10,2},{3,11},{11,3},{4,12},{12,4},... | collective-permute-start | bytes 1769480 | tf_op jit(solution)/shard_map/ppermute | solution.py:240
  131.6 47.7 %collective-permute-start.13 = (bf16[128,1152]{1,0:T(8,128)(2,1)}, bf16[128,1152]{1,0:T(8,128)(2,1)}, u32[]{:S(2)}, u32[]{:S(2)}) collective-permute-start(bf16[128,1152]{1,0:T(8,128)(2,1)} %get-tuple-element.207), channel_id=1, source_target_pairs={{0,3},{1,0},{2,1},{3,2},{4,7},{5,4},{6,5},{7,6},{8,11},{9,8},{10,9... | collective-permute-start | bytes 884744 | tf_op jit(solution)/shard_map/ppermute | solution.py:240
  133.5 59.6 %collective-permute-start.38 = (bf16[576,512]{1,0:T(8,128)(2,1)}, bf16[576,512]{1,0:T(8,128)(2,1)}, u32[]{:S(2)}, u32[]{:S(2)}) collective-permute-start(bf16[576,512]{1,0:T(8,128)(2,1)} %copy-done.82), channel_id=1, source_target_pairs={{0,8},{8,0},{1,9},{9,1},{2,10},{10,2},{3,11},{11,3},{4,12},{12,4},... | collective-permute-start | bytes 1769480 | tf_op jit(solution)/shard_map/ppermute | solution.py:240
  135.0 58.2 %collective-permute-start.39 = (bf16[576,512]{1,0:T(8,128)(2,1)}, bf16[576,512]{1,0:T(8,128)(2,1)}, u32[]{:S(2)}, u32[]{:S(2)}) collective-permute-start(bf16[576,512]{1,0:T(8,128)(2,1)} %copy-done.84), channel_id=1, source_target_pairs={{0,8},{8,0},{1,9},{9,1},{2,10},{10,2},{3,11},{11,3},{4,12},{12,4},... | collective-permute-start | bytes 1769480 | tf_op jit(solution)/shard_map/ppermute | solution.py:240
  137.2 56.5 %collective-permute-start.40 = (bf16[576,512]{1,0:T(8,128)(2,1)}, bf16[576,512]{1,0:T(8,128)(2,1)}, u32[]{:S(2)}, u32[]{:S(2)}) collective-permute-start(bf16[576,512]{1,0:T(8,128)(2,1)} %collective-permute-done.36), channel_id=1, source_target_pairs={{0,8},{8,0},{1,9},{9,1},{2,10},{10,2},{3,11},{11,3},{4,12},{12,4},... | collective-permute-start | bytes 1769480 | tf_op jit(solution)/shard_map/ppermute | solution.py:240
  172.2 20.4 %collective-permute-start.18 = (bf16[128,1152]{1,0:T(8,128)(2,1)}, bf16[128,1152]{1,0:T(8,128)(2,1)}, u32[]{:S(2)}, u32[]{:S(2)}) collective-permute-start(bf16[128,1152]{1,0:T(8,128)(2,1)} %copy-done.114), channel_id=1, source_target_pairs={{0,1},{1,2},{2,3},{3,0},{4,5},{5,6},{6,7},{7,4},{8,9},{9,10},{10,1... | collective-permute-start | bytes 884744 | tf_op jit(solution)/shard_map/ppermute | solution.py:240
  192.5 22.7 %collective-permute-start.16 = (bf16[128,1152]{1,0:T(8,128)(2,1)}, bf16[128,1152]{1,0:T(8,128)(2,1)}, u32[]{:S(2)}, u32[]{:S(2)}) collective-permute-start(bf16[128,1152]{1,0:T(8,128)(2,1)} %copy-done.114), channel_id=1, source_target_pairs={{0,4},{4,0},{1,5},{5,1},{2,6},{6,2},{3,7},{7,3},{8,12},{12,8},{9,1... | collective-permute-start | bytes 884744 | tf_op jit(solution)/shard_map/ppermute | solution.py:240
  192.6 35.7 %collective-permute-start.23 = (bf16[128,1152]{1,0:T(8,128)(2,1)}, bf16[128,1152]{1,0:T(8,128)(2,1)}, u32[]{:S(2)}, u32[]{:S(2)}) collective-permute-start(bf16[128,1152]{1,0:T(8,128)(2,1)} %collective-permute-done.13), channel_id=1, source_target_pairs={{0,4},{4,0},{1,5},{5,1},{2,6},{6,2},{3,7},{7,3},{8,12},{12,8},{9,1... | collective-permute-start | bytes 884744 | tf_op jit(solution)/shard_map/ppermute | solution.py:240
  193.1 28.6 %collective-permute-start.19 = (bf16[128,1152]{1,0:T(8,128)(2,1)}, bf16[128,1152]{1,0:T(8,128)(2,1)}, u32[]{:S(2)}, u32[]{:S(2)}) collective-permute-start(bf16[128,1152]{1,0:T(8,128)(2,1)} %collective-permute-done.18), channel_id=1, source_target_pairs={{0,4},{4,0},{1,5},{5,1},{2,6},{6,2},{3,7},{7,3},{8,12},{12,8},{9,1... | collective-permute-start | bytes 884744 | tf_op jit(solution)/shard_map/ppermute | solution.py:240
  193.1 22.6 %collective-permute-start.21 = (bf16[128,1152]{1,0:T(8,128)(2,1)}, bf16[128,1152]{1,0:T(8,128)(2,1)}, u32[]{:S(2)}, u32[]{:S(2)}) collective-permute-start(bf16[128,1152]{1,0:T(8,128)(2,1)} %collective-permute-done.18), channel_id=1, source_target_pairs={{0,1},{1,2},{2,3},{3,0},{4,5},{5,6},{6,7},{7,4},{8,9},{9,10},{10,1... | collective-permute-start | bytes 884744 | tf_op jit(solution)/shard_map/ppermute | solution.py:240
  193.7 19.9 %collective-permute-start.15 = (bf16[128,1152]{1,0:T(8,128)(2,1)}, bf16[128,1152]{1,0:T(8,128)(2,1)}, u32[]{:S(2)}, u32[]{:S(2)}) collective-permute-start(bf16[128,1152]{1,0:T(8,128)(2,1)} %collective-permute-done.14), channel_id=1, source_target_pairs={{0,3},{1,0},{2,1},{3,2},{4,7},{5,4},{6,5},{7,6},{8,11},{9,8},{10,9... | collective-permute-start | bytes 884744 | tf_op jit(solution)/shard_map/ppermute | solution.py:240
  295.3 21.4 %collective-permute-start.55 = (bf16[4,128,2,448]{1,3,2,0:T(8,128)(2,1)}, bf16[4,128,2,448]{1,3,2,0:T(8,128)(2,1)}, u32[]{:S(2)}, u32[]{:S(2)}) collective-permute-start(bf16[4,128,2,448]{1,3,2,0:T(8,128)(2,1)} %get-tuple-element.198), channel_id=1, source_target_pairs={{0,4},{4,0},{1,5},{5,1},{2,6},{6,2},{3,7},{7,3},{8,12},{12,8},{9,1... | collective-permute-start | bytes 2752520 | tf_op jit(solution)/shard_map/ppermute | solution.py:240
  322.0 50.4 %collective-permute-start.56 = (bf16[2,4,128,896]{3,2,0,1:T(8,128)(2,1)}, bf16[2,4,128,896]{3,2,0,1:T(8,128)(2,1)}, u32[]{:S(2)}, u32[]{:S(2)}) collective-permute-start(bf16[2,4,128,896]{3,2,0,1:T(8,128)(2,1)} %pad_maximum_fusion.12), channel_id=1, source_target_pairs={{0,8},{8,0},{1,9},{9,1},{2,10},{10,2},{3,11},{11,3},{4,12},{12,4},... | collective-permute-start | bytes 5505032 | tf_op jit(solution)/shard_map/ppermute | solution.py:240
  368.6 18.4 %collective-permute-start.41 = (bf16[128,1024]{1,0:T(8,128)(2,1)}, bf16[128,1024]{1,0:T(8,128)(2,1)S(1)}, u32[]{:S(2)}, u32[]{:S(2)}) collective-permute-start(bf16[128,1024]{1,0:T(8,128)(2,1)} %get-tuple-element.278), channel_id=1, source_target_pairs={{0,4},{4,0},{1,5},{5,1},{2,6},{6,2},{3,7},{7,3},{8,12},{12,8},{9,1... | collective-permute-start | bytes 786440 | tf_op jit(solution)/shard_map/ppermute | solution.py:240
  485.1 23.7 %collective-permute-start.68 = (bf16[128,1024]{1,0:T(8,128)(2,1)}, bf16[128,1024]{1,0:T(8,128)(2,1)}, u32[]{:S(2)}, u32[]{:S(2)}) collective-permute-start(bf16[128,1024]{1,0:T(8,128)(2,1)} %get-tuple-element.274), channel_id=1, source_target_pairs={{0,4},{4,0},{1,5},{5,1},{2,6},{6,2},{3,7},{7,3},{8,12},{12,8},{9,1... | collective-permute-start | bytes 786440 | tf_op jit(solution)/shard_map/ppermute | solution.py:240
  485.1 23.7 %collective-permute-start.70 = (bf16[128,1024]{1,0:T(8,128)(2,1)}, bf16[128,1024]{1,0:T(8,128)(2,1)}, u32[]{:S(2)}, u32[]{:S(2)}) collective-permute-start(bf16[128,1024]{1,0:T(8,128)(2,1)} %get-tuple-element.274), channel_id=1, source_target_pairs={{0,1},{1,2},{2,3},{3,0},{4,5},{5,6},{6,7},{7,4},{8,9},{9,10},{10,1... | collective-permute-start | bytes 786440 | tf_op jit(solution)/shard_map/ppermute | solution.py:240
  494.0 23.8 %collective-permute-start.173 = (bf16[128,4,2,2,128]{4,3,2,1,0:T(2,128)(2,1)S(1)}, bf16[128,4,2,2,128]{4,3,2,1,0:T(2,128)(2,1)S(1)}, u32[]{:S(2)}, u32[]{:S(2)}) collective-permute-start(bf16[128,4,2,2,128]{4,3,2,1,0:T(2,128)(2,1)S(1)} %fusion.97), channel_id=1, source_target_pairs={{0,8},{8,0},{1,9},{9,1},{2,10},{10,2},{3,11},{11,3},{4,12},{12,4},... | collective-permute-start | bytes 1572872 | tf_op jit(solution)/shard_map/ppermute | solution.py:240
  508.8 52.4 %collective-permute-start.74 = (bf16[128,1024]{1,0:T(8,128)(2,1)}, bf16[128,1024]{1,0:T(8,128)(2,1)}, u32[]{:S(2)}, u32[]{:S(2)}) collective-permute-start(bf16[128,1024]{1,0:T(8,128)(2,1)} %collective-permute-done.70), channel_id=1, source_target_pairs={{0,4},{4,0},{1,5},{5,1},{2,6},{6,2},{3,7},{7,3},{8,12},{12,8},{9,1... | collective-permute-start | bytes 786440 | tf_op jit(solution)/shard_map/ppermute | solution.py:240
  511.0 26.9 %collective-permute-start.76 = (bf16[128,1024]{1,0:T(8,128)(2,1)}, bf16[128,1024]{1,0:T(8,128)(2,1)S(1)}, u32[]{:S(2)}, u32[]{:S(2)}) collective-permute-start(bf16[128,1024]{1,0:T(8,128)(2,1)} %collective-permute-done.70), channel_id=1, source_target_pairs={{0,1},{1,2},{2,3},{3,0},{4,5},{5,6},{6,7},{7,4},{8,9},{9,10},{10,1... | collective-permute-start | bytes 786440 | tf_op jit(solution)/shard_map/ppermute | solution.py:240
  513.8 30.3 %collective-permute-start.72 = (bf16[128,1024]{1,0:T(8,128)(2,1)}, bf16[128,1024]{1,0:T(8,128)(2,1)S(1)}, u32[]{:S(2)}, u32[]{:S(2)}) collective-permute-start(bf16[128,1024]{1,0:T(8,128)(2,1)} %collective-permute-done.71), channel_id=1, source_target_pairs={{0,3},{1,0},{2,1},{3,2},{4,7},{5,4},{6,5},{7,6},{8,11},{9,8},{10,9... | collective-permute-start | bytes 786440 | tf_op jit(solution)/shard_map/ppermute | solution.py:240
  537.9 26.2 %collective-permute-start.81 = (bf16[128,1024]{1,0:T(8,128)(2,1)}, bf16[128,1024]{1,0:T(8,128)(2,1)S(1)}, u32[]{:S(2)}, u32[]{:S(2)}) collective-permute-start(bf16[128,1024]{1,0:T(8,128)(2,1)} %collective-permute-done.71), channel_id=1, source_target_pairs={{0,4},{4,0},{1,5},{5,1},{2,6},{6,2},{3,7},{7,3},{8,12},{12,8},{9,1... | collective-permute-start | bytes 786440 | tf_op jit(solution)/shard_map/ppermute | solution.py:240
  542.5 20.4 %collective-permute-start.77 = (bf16[128,1024]{1,0:T(8,128)(2,1)S(1)}, bf16[128,1024]{1,0:T(8,128)(2,1)S(1)}, u32[]{:S(2)}, u32[]{:S(2)}) collective-permute-start(bf16[128,1024]{1,0:T(8,128)(2,1)S(1)} %collective-permute-done.76), channel_id=1, source_target_pairs={{0,4},{4,0},{1,5},{5,1},{2,6},{6,2},{3,7},{7,3},{8,12},{12,8},{9,1... | collective-permute-start | bytes 786440 | tf_op jit(solution)/shard_map/ppermute | solution.py:240
  544.1 17.7 %collective-permute-start.79 = (bf16[128,1024]{1,0:T(8,128)(2,1)S(1)}, bf16[128,1024]{1,0:T(8,128)(2,1)S(1)}, u32[]{:S(2)}, u32[]{:S(2)}) collective-permute-start(bf16[128,1024]{1,0:T(8,128)(2,1)S(1)} %collective-permute-done.76), channel_id=1, source_target_pairs={{0,1},{1,2},{2,3},{3,0},{4,5},{5,6},{6,7},{7,4},{8,9},{9,10},{10,1... | collective-permute-start | bytes 786440 | tf_op jit(solution)/shard_map/ppermute | solution.py:240
  652.7 27.3 %collective-permute-start.92 = (f32[2,1024]{1,0:T(2,128)S(1)}, f32[2,1024]{1,0:T(2,128)S(1)}, u32[]{:S(2)}, u32[]{:S(2)}) collective-permute-start(f32[2,1024]{1,0:T(2,128)S(1)} %pad_maximum_fusion.32), channel_id=1, source_target_pairs={{0,4},{4,0},{1,5},{5,1},{2,6},{6,2},{3,7},{7,3},{8,12},{12,8},{9,1... | collective-permute-start | bytes 24584 | tf_op jit(solution)/shard_map/ppermute | solution.py:240
  679.4 53.0 %collective-permute-start.162 = (bf16[448,4,2,2,128]{4,3,2,1,0:T(2,128)(2,1)}, bf16[448,4,2,2,128]{4,3,2,1,0:T(2,128)(2,1)}, u32[]{:S(2)}, u32[]{:S(2)}) collective-permute-start(bf16[448,4,2,2,128]{4,3,2,1,0:T(2,128)(2,1)} %fusion.26), channel_id=1, source_target_pairs={{0,8},{8,0},{1,9},{9,1},{2,10},{10,2},{3,11},{11,3},{4,12},{12,4},... | collective-permute-start | bytes 5505032 | tf_op jit(solution)/shard_map/ppermute | solution.py:240
  681.5 17.5 %collective-permute-start.94 = (f32[2,1024]{1,0:T(2,128)S(1)}, f32[2,1024]{1,0:T(2,128)S(1)}, u32[]{:S(2)}, u32[]{:S(2)}) collective-permute-start(f32[2,1024]{1,0:T(2,128)S(1)} %fusion.145), channel_id=1, source_target_pairs={{0,2},{1,3},{2,0},{3,1},{4,6},{5,7},{6,4},{7,5},{8,10},{9,11},{10,... | collective-permute-start | bytes 24584 | tf_op jit(solution)/shard_map/ppermute | solution.py:240
  723.9 42.2 %collective-permute-start.170 = (bf16[8,128,896]{1,2,0:T(8,128)(2,1)}, bf16[8,128,896]{1,2,0:T(8,128)(2,1)S(1)}, u32[]{:S(2)}, u32[]{:S(2)}) collective-permute-start(bf16[8,128,896]{1,2,0:T(8,128)(2,1)} %bitcast.565), channel_id=1, source_target_pairs={{0,8},{8,0},{1,9},{9,1},{2,10},{10,2},{3,11},{11,3},{4,12},{12,4},... | collective-permute-start | bytes 5505032 | tf_op jit(solution)/shard_map/ppermute | solution.py:240
  723.9 53.1 %collective-permute-start.102 = (bf16[128,1024]{1,0:T(8,128)(2,1)}, bf16[128,1024]{1,0:T(8,128)(2,1)}, u32[]{:S(2)}, u32[]{:S(2)}) collective-permute-start(bf16[128,1024]{1,0:T(8,128)(2,1)} %collective-permute-done.98), channel_id=1, source_target_pairs={{0,4},{4,0},{1,5},{5,1},{2,6},{6,2},{3,7},{7,3},{8,12},{12,8},{9,1... | collective-permute-start | bytes 786440 | tf_op jit(solution)/shard_map/ppermute | solution.py:240
  725.7 51.8 %collective-permute-start.104 = (bf16[128,1024]{1,0:T(8,128)(2,1)}, bf16[128,1024]{1,0:T(8,128)(2,1)}, u32[]{:S(2)}, u32[]{:S(2)}) collective-permute-start(bf16[128,1024]{1,0:T(8,128)(2,1)} %collective-permute-done.98), channel_id=1, source_target_pairs={{0,1},{1,2},{2,3},{3,0},{4,5},{5,6},{6,7},{7,4},{8,9},{9,10},{10,1... | collective-permute-start | bytes 786440 | tf_op jit(solution)/shard_map/ppermute | solution.py:240
  726.6 42.3 %collective-permute-start.100 = (bf16[128,1024]{1,0:T(8,128)(2,1)}, bf16[128,1024]{1,0:T(8,128)(2,1)}, u32[]{:S(2)}, u32[]{:S(2)}) collective-permute-start(bf16[128,1024]{1,0:T(8,128)(2,1)} %collective-permute-done.99), channel_id=1, source_target_pairs={{0,3},{1,0},{2,1},{3,2},{4,7},{5,4},{6,5},{7,6},{8,11},{9,8},{10,9... | collective-permute-start | bytes 786440 | tf_op jit(solution)/shard_map/ppermute | solution.py:240
  732.4 64.6 %collective-permute-start.109 = (bf16[128,1024]{1,0:T(8,128)(2,1)}, bf16[128,1024]{1,0:T(8,128)(2,1)}, u32[]{:S(2)}, u32[]{:S(2)}) collective-permute-start(bf16[128,1024]{1,0:T(8,128)(2,1)} %collective-permute-done.99), channel_id=1, source_target_pairs={{0,4},{4,0},{1,5},{5,1},{2,6},{6,2},{3,7},{7,3},{8,12},{12,8},{9,1... | collective-permute-start | bytes 786440 | tf_op jit(solution)/shard_map/ppermute | solution.py:240
  776.4 210.6 %collective-permute-start.171 = (bf16[4,128,2,1,448]{1,4,3,2,0:T(8,128)(2,1)}, bf16[4,128,2,1,448]{1,4,3,2,0:T(8,128)(2,1)}, u32[]{:S(2)}, u32[]{:S(2)}) collective-permute-start(bf16[4,128,2,1,448]{1,4,3,2,0:T(8,128)(2,1)} %get-tuple-element.192), channel_id=1, source_target_pairs={{0,4},{4,0},{1,5},{5,1},{2,6},{6,2},{3,7},{7,3},{8,12},{12,8},{9,1... | collective-permute-start | bytes 2752520 | tf_op jit(solution)/shard_map/ppermute | solution.py:240
  786.0 188.8 %collective-permute-start.164 = (bf16[448,512]{1,0:T(8,128)(2,1)}, bf16[448,512]{1,0:T(8,128)(2,1)}, u32[]{:S(2)}, u32[]{:S(2)}) collective-permute-start(bf16[448,512]{1,0:T(8,128)(2,1)} %squeeze.442), channel_id=1, source_target_pairs={{0,3},{1,0},{2,1},{3,2},{4,7},{5,4},{6,5},{7,6},{8,11},{9,8},{10,9... | collective-permute-start | bytes 1376264 | tf_op jit(solution)/shard_map/ppermute | solution.py:240
  790.5 187.8 %collective-permute-start.166 = (bf16[448,512]{1,0:T(8,128)(2,1)}, bf16[448,512]{1,0:T(8,128)(2,1)}, u32[]{:S(2)}, u32[]{:S(2)}) collective-permute-start(bf16[448,512]{1,0:T(8,128)(2,1)} %squeeze.443), channel_id=1, source_target_pairs={{0,2},{1,3},{2,0},{3,1},{4,6},{5,7},{6,4},{7,5},{8,10},{9,11},{10,... | collective-permute-start | bytes 1376264 | tf_op jit(solution)/shard_map/ppermute | solution.py:240
  796.2 185.8 %collective-permute-start.168 = (bf16[448,512]{1,0:T(8,128)(2,1)}, bf16[448,512]{1,0:T(8,128)(2,1)}, u32[]{:S(2)}, u32[]{:S(2)}) collective-permute-start(bf16[448,512]{1,0:T(8,128)(2,1)} %squeeze.444), channel_id=1, source_target_pairs={{0,1},{1,2},{2,3},{3,0},{4,5},{5,6},{6,7},{7,4},{8,9},{9,10},{10,1... | collective-permute-start | bytes 1376264 | tf_op jit(solution)/shard_map/ppermute | solution.py:240
  983.7 21.9 %collective-permute-start.167 = (bf16[448,512]{1,0:T(8,128)(2,1)}, bf16[448,512]{1,0:T(8,128)(2,1)S(1)}, u32[]{:S(2)}, u32[]{:S(2)}) collective-permute-start(bf16[448,512]{1,0:T(8,128)(2,1)} %collective-permute-done.166), channel_id=1, source_target_pairs={{0,16},{16,0},{1,17},{17,1},{2,18},{18,2},{3,19},{19,3},{4,20},{20... | collective-permute-start | bytes 1376264 | tf_op jit(solution)/shard_map/ppermute | solution.py:240
  984.2 30.0 %collective-permute-start.169 = (bf16[448,512]{1,0:T(8,128)(2,1)}, bf16[448,512]{1,0:T(8,128)(2,1)S(1)}, u32[]{:S(2)}, u32[]{:S(2)}) collective-permute-start(bf16[448,512]{1,0:T(8,128)(2,1)} %collective-permute-done.168), channel_id=1, source_target_pairs={{0,16},{16,0},{1,17},{17,1},{2,18},{18,2},{3,19},{19,3},{4,20},{20... | collective-permute-start | bytes 1376264 | tf_op jit(solution)/shard_map/ppermute | solution.py:240
  985.8 33.2 %collective-permute-start.159 = (bf16[8,128,256]{1,2,0:T(8,128)(2,1)S(1)}, bf16[8,128,256]{1,2,0:T(8,128)(2,1)S(1)}, u32[]{:S(2)}, u32[]{:S(2)}) collective-permute-start(bf16[8,128,256]{1,2,0:T(8,128)(2,1)S(1)} %bitcast.573), channel_id=1, source_target_pairs={{0,8},{8,0},{1,9},{9,1},{2,10},{10,2},{3,11},{11,3},{4,12},{12,4},... | collective-permute-start | bytes 1572872 | tf_op jit(solution)/shard_map/ppermute | solution.py:240
  987.0 32.2 %collective-permute-start.151 = (bf16[128,4,2,2,128]{4,3,2,1,0:T(2,128)(2,1)}, bf16[128,4,2,2,128]{4,3,2,1,0:T(2,128)(2,1)S(1)}, u32[]{:S(2)}, u32[]{:S(2)}) collective-permute-start(bf16[128,4,2,2,128]{4,3,2,1,0:T(2,128)(2,1)} %fusion.96), channel_id=1, source_target_pairs={{0,8},{8,0},{1,9},{9,1},{2,10},{10,2},{3,11},{11,3},{4,12},{12,4},... | collective-permute-start | bytes 1572872 | tf_op jit(solution)/shard_map/ppermute | solution.py:240
  995.8 27.3 %collective-permute-start.143 = (bf16[128,4,2,2,128]{4,3,2,1,0:T(2,128)(2,1)}, bf16[128,4,2,2,128]{4,3,2,1,0:T(2,128)(2,1)S(1)}, u32[]{:S(2)}, u32[]{:S(2)}) collective-permute-start(bf16[128,4,2,2,128]{4,3,2,1,0:T(2,128)(2,1)} %fusion.95), channel_id=1, source_target_pairs={{0,8},{8,0},{1,9},{9,1},{2,10},{10,2},{3,11},{11,3},{4,12},{12,4},... | collective-permute-start | bytes 1572872 | tf_op jit(solution)/shard_map/ppermute | solution.py:240
  1005.6 28.7 %collective-permute-start.135 = (bf16[128,4,2,2,128]{4,3,2,1,0:T(2,128)(2,1)S(1)}, bf16[128,4,2,2,128]{4,3,2,1,0:T(2,128)(2,1)S(1)}, u32[]{:S(2)}, u32[]{:S(2)}) collective-permute-start(bf16[128,4,2,2,128]{4,3,2,1,0:T(2,128)(2,1)S(1)} %copy-done.104), channel_id=1, source_target_pairs={{0,8},{8,0},{1,9},{9,1},{2,10},{10,2},{3,11},{11,3},{4,12},{12,4},... | collective-permute-start | bytes 1572872 | tf_op jit(solution)/shard_map/ppermute | solution.py:240
  1014.2 29.3 %collective-permute-start.127 = (bf16[128,4,2,2,128]{4,3,2,1,0:T(2,128)(2,1)S(1)}, bf16[128,4,2,2,128]{4,3,2,1,0:T(2,128)(2,1)S(1)}, u32[]{:S(2)}, u32[]{:S(2)}) collective-permute-start(bf16[128,4,2,2,128]{4,3,2,1,0:T(2,128)(2,1)S(1)} %copy-done.103), channel_id=1, source_target_pairs={{0,8},{8,0},{1,9},{9,1},{2,10},{10,2},{3,11},{11,3},{4,12},{12,4},... | collective-permute-start | bytes 1572872 | tf_op jit(solution)/shard_map/ppermute | solution.py:240
  1019.0 46.9 %collective-permute-start.110 = (bf16[2,128,1152]{2,1,0:T(8,128)(2,1)}, bf16[2,128,1152]{2,1,0:T(8,128)(2,1)}, u32[]{:S(2)}, u32[]{:S(2)}) collective-permute-start(bf16[2,128,1152]{2,1,0:T(8,128)(2,1)} %get-tuple-element.148), channel_id=1, source_target_pairs={{0,4},{4,0},{1,5},{5,1},{2,6},{6,2},{3,7},{7,3},{8,12},{12,8},{9,1... | collective-permute-start | bytes 1769480 | tf_op jit(solution)/shard_map/ppermute | solution.py:240
  1019.2 46.8 %collective-permute-start.112 = (bf16[2,128,1152]{2,1,0:T(8,128)(2,1)}, bf16[2,128,1152]{2,1,0:T(8,128)(2,1)}, u32[]{:S(2)}, u32[]{:S(2)}) collective-permute-start(bf16[2,128,1152]{2,1,0:T(8,128)(2,1)} %get-tuple-element.147), channel_id=1, source_target_pairs={{0,4},{4,0},{1,5},{5,1},{2,6},{6,2},{3,7},{7,3},{8,12},{12,8},{9,1... | collective-permute-start | bytes 1769480 | tf_op jit(solution)/shard_map/ppermute | solution.py:240
  1023.1 44.5 %collective-permute-start.114 = (bf16[2,128,1152]{2,1,0:T(8,128)(2,1)}, bf16[2,128,1152]{2,1,0:T(8,128)(2,1)}, u32[]{:S(2)}, u32[]{:S(2)}) collective-permute-start(bf16[2,128,1152]{2,1,0:T(8,128)(2,1)} %get-tuple-element.145), channel_id=1, source_target_pairs={{0,4},{4,0},{1,5},{5,1},{2,6},{6,2},{3,7},{7,3},{8,12},{12,8},{9,1... | collective-permute-start | bytes 1769480 | tf_op jit(solution)/shard_map/ppermute | solution.py:240
  1034.3 34.8 %collective-permute-start.116 = (bf16[2,128,1152]{2,1,0:T(8,128)(2,1)}, bf16[2,128,1152]{2,1,0:T(8,128)(2,1)}, u32[]{:S(2)}, u32[]{:S(2)}) collective-permute-start(bf16[2,128,1152]{2,1,0:T(8,128)(2,1)} %get-tuple-element.146), channel_id=1, source_target_pairs={{0,4},{4,0},{1,5},{5,1},{2,6},{6,2},{3,7},{7,3},{8,12},{12,8},{9,1... | collective-permute-start | bytes 1769480 | tf_op jit(solution)/shard_map/ppermute | solution.py:240
  1043.4 165.8 %collective-permute-start.172 = (bf16[4,128,1792]{1,2,0:T(8,128)(2,1)}, bf16[4,128,1792]{1,2,0:T(8,128)(2,1)}, u32[]{:S(2)}, u32[]{:S(2)}) collective-permute-start(bf16[4,128,1792]{1,2,0:T(8,128)(2,1)} %bitcast.200), channel_id=1, source_target_pairs={{0,16},{16,0},{1,17},{17,1},{2,18},{18,2},{3,19},{19,3},{4,20},{20... | collective-permute-start | bytes 5505032 | tf_op jit(solution)/shard_map/ppermute | solution.py:240
  1065.9 38.6 %collective-permute-start.160 = (bf16[4,128,2,1,128]{4,1,3,2,0:T(8,128)(2,1)}, bf16[4,128,2,1,128]{4,1,3,2,0:T(8,128)(2,1)S(1)}, u32[]{:S(2)}, u32[]{:S(2)}) collective-permute-start(bf16[4,128,2,1,128]{4,1,3,2,0:T(8,128)(2,1)} %bitcast.185), channel_id=1, source_target_pairs={{0,4},{4,0},{1,5},{5,1},{2,6},{6,2},{3,7},{7,3},{8,12},{12,8},{9,1... | collective-permute-start | bytes 786440 | tf_op jit(solution)/shard_map/ppermute | solution.py:240
  1066.0 20.6 %collective-permute-start.152 = (bf16[128,512]{1,0:T(8,128)(2,1)}, bf16[128,512]{1,0:T(8,128)(2,1)S(1)}, u32[]{:S(2)}, u32[]{:S(2)}) collective-permute-start(bf16[128,512]{1,0:T(8,128)(2,1)} %squeeze.433), channel_id=1, source_target_pairs={{0,16},{16,0},{1,17},{17,1},{2,18},{18,2},{3,19},{19,3},{4,20},{20... | collective-permute-start | bytes 393224 | tf_op jit(solution)/shard_map/ppermute | solution.py:240
  1067.6 31.9 %collective-permute-start.153 = (bf16[128,512]{1,0:T(8,128)(2,1)}, bf16[128,512]{1,0:T(8,128)(2,1)}, u32[]{:S(2)}, u32[]{:S(2)}) collective-permute-start(bf16[128,512]{1,0:T(8,128)(2,1)} %squeeze.434), channel_id=1, source_target_pairs={{0,3},{1,0},{2,1},{3,2},{4,7},{5,4},{6,5},{7,6},{8,11},{9,8},{10,9... | collective-permute-start | bytes 393224 | tf_op jit(solution)/shard_map/ppermute | solution.py:240
  1069.1 39.7 %collective-permute-start.155 = (bf16[128,512]{1,0:T(8,128)(2,1)}, bf16[128,512]{1,0:T(8,128)(2,1)}, u32[]{:S(2)}, u32[]{:S(2)}) collective-permute-start(bf16[128,512]{1,0:T(8,128)(2,1)} %squeeze.435), channel_id=1, source_target_pairs={{0,2},{1,3},{2,0},{3,1},{4,6},{5,7},{6,4},{7,5},{8,10},{9,11},{10,... | collective-permute-start | bytes 393224 | tf_op jit(solution)/shard_map/ppermute | solution.py:240
  1112.9 17.2 %collective-permute-start.149 = (bf16[128,512]{1,0:T(8,128)(2,1)}, bf16[128,512]{1,0:T(8,128)(2,1)S(1)}, u32[]{:S(2)}, u32[]{:S(2)}) collective-permute-start(bf16[128,512]{1,0:T(8,128)(2,1)} %squeeze.431), channel_id=1, source_target_pairs={{0,1},{1,2},{2,3},{3,0},{4,5},{5,6},{6,7},{7,4},{8,9},{9,10},{10,1... | collective-permute-start | bytes 393224 | tf_op jit(solution)/shard_map/ppermute | solution.py:240
  1140.4 17.3 %collective-permute-start.131 = (bf16[128,512]{1,0:T(8,128)(2,1)S(1)}, bf16[128,512]{1,0:T(8,128)(2,1)S(1)}, u32[]{:S(2)}, u32[]{:S(2)}) collective-permute-start(bf16[128,512]{1,0:T(8,128)(2,1)S(1)} %copy-done.128), channel_id=1, source_target_pairs={{0,2},{1,3},{2,0},{3,1},{4,6},{5,7},{6,4},{7,5},{8,10},{9,11},{10,... | collective-permute-start | bytes 393224 | tf_op jit(solution)/shard_map/ppermute | solution.py:240
  1163.6 21.9 %collective-permute-start.161 = (bf16[4,128,512]{1,2,0:T(8,128)(2,1)S(1)}, bf16[4,128,512]{1,2,0:T(8,128)(2,1)S(1)}, u32[]{:S(2)}, u32[]{:S(2)}) collective-permute-start(bf16[4,128,512]{1,2,0:T(8,128)(2,1)S(1)} %bitcast.563), channel_id=1, source_target_pairs={{0,16},{16,0},{1,17},{17,1},{2,18},{18,2},{3,19},{19,3},{4,20},{20... | collective-permute-start | bytes 1572872 | tf_op jit(solution)/shard_map/ppermute | solution.py:240
  (277 other events, 5834.1 us)
